TPU v7x, 512 devices: a whole 4x8x8 slice. The times are simulated.
512 devices in a mesh: row: 64 (over z, y), col: 8 (over x, core).
Axes of the slice: x: 4, y: 8, z: 8, core: 2. Of those that a mesh axis runs over, the one named last changes fastest.
Arguments:
- dinv0: bfloat16 [65536, 4096], P('row', 'col'), as said below
- dinv1: bfloat16 [32768, 4096], P('row', 'col'), as said below
- dinv2: bfloat16 [16384, 4096], P('row', 'col'), as said below
- offdiag0: bfloat16 [65536, 4096], P('row', 'col'), may hold values from -0.0625 to 0.0625
- offdiag1: bfloat16 [32768, 4096], P('row', 'col'), may hold values from -0.0625 to 0.0625
- rhs0: bfloat16 [65536, 128], P(('row', 'col')), may hold values from -6 to 6
- rhs1: bfloat16 [32768, 128], P(('row', 'col')), may hold values from -6 to 6
- rhs2: bfloat16 [16384, 128], P(('row', 'col')), may hold values from -6 to 6
- block_rows0: int32 [16, 64, 16], replicated, may hold values from 0 to 63, all different within a row
- block_rows1: int32 [8, 64, 16], replicated, may hold values from 0 to 63, all different within a row
Outputs:
- solution0: float32 [65536, 128], P(('row', 'col'))
- solution1: float32 [32768, 128], P(('row', 'col'))
- solution2: float32 [16384, 128], P(('row', 'col'))
Inputs may be any that keep to these rules, and one draw needn't show every extreme that they name: `block_rows0`: each row of the last dimension lists 16 different block rows. `block_rows1`: each row of the last dimension lists 16 different block rows. `dinv0`: each supernode's block is lower triangular in global order, with a positive diagonal. `dinv1`: each supernode's block is lower triangular in global order, with a positive diagonal. `dinv2`: each supernode's block is lower triangular in global order, with a positive diagonal.
All inputs are finite; a program needn't handle non-finite values.
Results may differ from a plain program's by a relative error of at most 0.0095.
Values may be sent and summed in bfloat16 or wider, within the bound.
No kernel may reach another device: no remote copies, remote signals or barrier semaphores. Data moves between devices by JAX's collectives and lax.ppermute only.
A program may use at most 64 MiB of HBM per device.

v0:
```python
import jax
import jax.numpy as jnp
from jax import lax
from jax.sharding import PartitionSpec as P

MB = 64
GR = 4


def partner(value, axis, stride):
    return lax.ppermute(value, axis, [(i, i ^ 1 << stride) for i in range(lax.axis_size(axis))])


def own_bit(which):
    return lax.axis_index("row") >> which & 1


def row_join(pieces, depth):
    joined = pieces
    for which in range(depth):
        other = partner(joined, "row", which)
        first = jnp.concatenate((joined, other), axis=1)
        second = jnp.concatenate((other, joined), axis=1)
        joined = jnp.where(own_bit(which) == 0, first, second)
    return joined.reshape(-1, joined.shape[-1])


def row_fold(partial_value, row_blocks, depth):
    width = partial_value.shape[-1]
    folded = partial_value.reshape(row_blocks, 1 << depth, -1, width)
    for which in range(depth):
        halves = folded.reshape(row_blocks, folded.shape[1] // 2, 2, folded.shape[2], width)
        mine = own_bit(which)
        keeping = lax.dynamic_index_in_dim(halves, mine, 2, keepdims=False)
        sending = lax.dynamic_index_in_dim(halves, 1 - mine, 2, keepdims=False)
        folded = keeping + partner(sending.astype(jnp.bfloat16), "row", which).astype(sending.dtype)
    return folded


def column_sum(partial_value, col_devs):
    width = partial_value.shape[-1]
    shaped = partial_value.reshape(-1, col_devs, MB // col_devs, width)
    return lax.psum_scatter(shaped, "col", scatter_dimension=1, tiled=True)


def column_join(pieces):
    gathered = lax.all_gather(pieces, "col", axis=1, tiled=True)
    return gathered.reshape(-1, gathered.shape[-1])


def sibling_fold(values, which):
    mine = own_bit(which)
    keeping = lax.dynamic_index_in_dim(values, mine, 1, keepdims=True)
    sending = lax.dynamic_index_in_dim(values, 1 - mine, 1, keepdims=True)
    return keeping + partner(sending.astype(jnp.bfloat16), "row", which).astype(sending.dtype)


def parent_rows(values, which):
    other = partner(values, "row", which)
    first = jnp.concatenate((values, other), axis=1)
    second = jnp.concatenate((other, values), axis=1)
    joined = jnp.where(own_bit(which) == 0, first, second)
    return joined.reshape(joined.shape[0] * 2, 1, joined.shape[2], joined.shape[3])


def coupling(values, listings, depth):
    row_count = values.shape[0]
    row_blocks = row_count // MB
    group = 1 << depth
    position = lax.axis_index("row")
    member = position // group
    local = position % group
    owned = jnp.arange(row_blocks, dtype=jnp.int32) * group + local
    listing = lax.dynamic_index_in_dim(listings, member, 0, keepdims=False)
    listed = jnp.any(listing[None, :, :] == owned[:, None, None], axis=-1)
    unit_width = values.shape[1] // listed.shape[1]
    keeping = jnp.repeat(jnp.repeat(listed, MB, axis=0), unit_width, axis=1)
    return jnp.where(keeping, values, jnp.zeros_like(values))


def per_device(dinv0, dinv1, dinv2, offdiag0, offdiag1, rhs0, rhs1, rhs2, block_rows0, block_rows1):
    col_devs = lax.axis_size("col")
    col_width = MB // col_devs
    width = rhs0.shape[1]
    lowest = GR.bit_length() - 1
    depths = (lowest, lowest + 1, lowest + 2)
    inverses = (dinv0, dinv1, dinv2)
    couplings = (
        coupling(offdiag0, block_rows0, depths[0]),
        coupling(offdiag1, block_rows1, depths[1]),
    )
    sides = (rhs0, rhs1, rhs2)

    def as_pieces(values):
        return values.reshape(-1, 1, col_width, width)

    solved = []
    residual = as_pieces(rhs0)
    for level in range(3):
        column_form = row_join(residual, depths[level])
        product = jnp.dot(inverses[level], column_form, preferred_element_type=jnp.float32)
        solved_pieces = column_sum(product, col_devs).astype(jnp.bfloat16)
        solved.append(solved_pieces)
        if level < 2:
            solved_columns = row_join(solved_pieces, depths[level])
            partial_value = jnp.dot(
                couplings[level], solved_columns, preferred_element_type=jnp.float32
            )
            summed = column_sum(partial_value, col_devs)
            summed = summed.reshape(summed.shape[0] // 2, 2, col_width, width)
            update = sibling_fold(summed, depths[level])
            residual = (as_pieces(sides[level + 1]).astype(jnp.float32) - update).astype(
                jnp.bfloat16
            )
    outputs = [None, None, None]
    weighted = solved[2]
    for level in (2, 1, 0):
        row_form = column_join(weighted)
        product = jnp.einsum(
            "ij,in->jn", inverses[level], row_form, preferred_element_type=jnp.float32
        )
        answer = row_fold(product, row_form.shape[0] // MB, depths[level])
        outputs[level] = answer.reshape(-1, width)
        if level > 0:
            child_pieces = parent_rows(answer.astype(jnp.bfloat16), depths[level - 1])
            child_form = column_join(child_pieces)
            partial_value = jnp.einsum(
                "ij,in->jn", couplings[level - 1], child_form, preferred_element_type=jnp.float32
            )
            carried = row_fold(partial_value, child_form.shape[0] // MB, depths[level - 1])
            weighted = (solved[level - 1].astype(jnp.float32) - carried).astype(jnp.bfloat16)
    return (outputs[0], outputs[1], outputs[2])


def solution(mesh):
    placed = (
        P("row", "col"),
        P("row", "col"),
        P("row", "col"),
        P("row", "col"),
        P("row", "col"),
        P(("row", "col"), None),
        P(("row", "col"), None),
        P(("row", "col"), None),
        P(),
        P(),
    )
    return jax.shard_map(
        per_device,
        mesh=mesh,
        in_specs=placed,
        out_specs=(P(("row", "col"), None), P(("row", "col"), None), P(("row", "col"), None)),
        check_vma=False,
    )
```

profile of v0, /device:TPU:24, one launch (start us, length us, event | category | flops | bytes accessed | tf_op | source)
XLA Modules:
  0.0 549.9 jit_solution(3072285865795595267)
XLA Ops:
  13.4 6.0 %collective-permute-start.1 = (bf16[16,2,8,128]{3,2,1,0:T(8,128)(2,1)S(1)}, bf16[16,2,8,128]{3,2,1,0:T(8,128)(2,1)S(1)}, u32[]{:S(2)}, u32[]{:S(2)}) collective-permute-start(bf16[16,2,8,128]{3,2,1,0:T(8,128)(2,1)S(1)} %maximum_select_fusion.5), channel_id=1, source_target_pairs={{0,16},{8,24},{16,0},{24,8},{32,48},{40,56},{48,32},{56,40},{64,80... | collective-permute-start | bytes 196616 | tf_op jit(solution)/shard_map/ppermute | solution.py:11
  22.4 29.2 %all-reduce.14 = bf16[16,8,8,128]{3,2,1,0:T(8,128)(2,1)S(1)} all-reduce(f32[16,8,8,128]{3,2,1,0:T(8,128)S(1)} %bitcast.169), channel_id=2, replica_groups=mesh['row'=64,'col'=8] {'col'}, use_global_device_ids=true, to_apply=%region_0.1.clone | all-reduce | flops 131072 | bytes 786432
  58.5 4.8 collective-permute-start.3
  66.9 73.2 %all-reduce.11.cloned.1.call-done = f32[16,8,8,128]{3,2,1,0:T(8,128)} async-done(((f32[16,8,8,128]{3,2,1,0:T(8,128)}), f32[16,8,8,128]{3,2,1,0:T(8,128)}) %all-reduce.11.cloned.1.call-update) | async-done | bytes 524304
  146.2 4.9 collective-permute-done.4
  174.0 26.3 %all-reduce.15 = bf16[8,8,8,128]{3,2,1,0:T(8,128)(2,1)S(1)} all-reduce(f32[8,8,8,128]{3,2,1,0:T(8,128)S(1)} %bitcast.170), channel_id=4, replica_groups=mesh['row'=64,'col'=8] {'col'}, use_global_device_ids=true, to_apply=%region_3.4.clone | all-reduce | flops 65536 | bytes 393216
  213.3 5.6 %collective-permute-start.10 = (bf16[8,4,8,128]{3,2,1,0:T(8,128)(2,1)S(1)}, bf16[8,4,8,128]{3,2,1,0:T(8,128)(2,1)S(1)}, u32[]{:S(2)}, u32[]{:S(2)}) collective-permute-start(bf16[8,4,8,128]{3,2,1,0:T(8,128)(2,1)S(1)} %maximum_select_fusion.8), channel_id=1, source_target_pairs={{0,32},{8,40},{16,48},{24,56},{32,0},{40,8},{48,16},{56,24},{64,96... | collective-permute-start | bytes 196616 | tf_op jit(solution)/shard_map/ppermute | solution.py:11
  225.5 72.1 %all-reduce.13.cloned.1.call-done = f32[8,8,8,128]{3,2,1,0:T(8,128)} async-done(((f32[8,8,8,128]{3,2,1,0:T(8,128)}), f32[8,8,8,128]{3,2,1,0:T(8,128)}) %all-reduce.13.cloned.1.call-update) | async-done | bytes 262160
  321.6 5.2 collective-permute-done.14
  334.9 25.3 %all-reduce.16 = bf16[4,8,8,128]{3,2,1,0:T(8,128)(2,1)} all-reduce(f32[4,8,8,128]{3,2,1,0:T(8,128)S(1)} %bitcast.183), channel_id=6, replica_groups=mesh['row'=64,'col'=8] {'col'}, use_global_device_ids=true, to_apply=%region_6.7.clone | all-reduce | flops 32768 | bytes 196608
  361.5 11.2 %all_gather.15 = bf16[4,8,8,128]{3,2,1,0:T(8,128)(2,1)S(1)} all-gather(bf16[4,1,8,128]{3,2,1,0:T(8,128)(2,1)S(1)} %dynamic-slice_convert_fusion.14), channel_id=1, replica_groups=mesh['row'=64,'col'=8] {'col'}, dimensions={1}, use_global_device_ids=true | all-gather | bytes 73728 | tf_op jit(solution)/shard_map/all_gather | solution.py:47
  384.2 4.8 collective-permute-done.17
  393.2 5.4 collective-permute-done.18
  410.3 11.3 %all_gather.16 = bf16[8,8,8,128]{3,2,1,0:T(8,128)(2,1)S(1)} all-gather(bf16[8,1,8,128]{3,2,1,0:T(8,128)(2,1)S(1)} %bitcast.201), channel_id=1, replica_groups=mesh['row'=64,'col'=8] {'col'}, dimensions={1}, use_global_device_ids=true | all-gather | bytes 147456 | tf_op jit(solution)/shard_map/all_gather | solution.py:47
  430.1 5.1 collective-permute-done.22
  439.1 5.7 %collective-permute-done.23 = bf16[8,1,8,128]{3,2,1,0:T(8,128)(2,1)S(1)} collective-permute-done((bf16[8,1,8,128]{3,2,1,0:T(8,128)(2,1)S(1)}, bf16[8,1,8,128]{3,2,1,0:T(8,128)(2,1)S(1)}, u32[]{:S(2)}, u32[]{:S(2)}) %collective-permute-start.23) | collective-permute-done | bytes 16416 | tf_op jit(solution)/shard_map/ppermute | solution.py:11
  446.2 11.3 %all_gather.17 = bf16[8,8,8,128]{3,2,1,0:T(8,128)(2,1)S(1)} all-gather(bf16[8,1,8,128]{3,2,1,0:T(8,128)(2,1)S(1)} %subtract_convert_fusion.1), channel_id=1, replica_groups=mesh['row'=64,'col'=8] {'col'}, dimensions={1}, use_global_device_ids=true | all-gather | bytes 147456 | tf_op jit(solution)/shard_map/all_gather | solution.py:47
  466.1 4.9 collective-permute-done.25
  474.8 5.8 %collective-permute-done.26 = bf16[8,1,8,128]{3,2,1,0:T(8,128)(2,1)S(1)} collective-permute-done((bf16[8,1,8,128]{3,2,1,0:T(8,128)(2,1)S(1)}, bf16[8,1,8,128]{3,2,1,0:T(8,128)(2,1)S(1)}, u32[]{:S(2)}, u32[]{:S(2)}) %collective-permute-start.26) | collective-permute-done | bytes 16416 | tf_op jit(solution)/shard_map/ppermute | solution.py:11
  484.9 5.8 %collective-permute-done.27 = bf16[8,1,8,128]{3,2,1,0:T(8,128)(2,1)S(1)} collective-permute-done((bf16[8,1,8,128]{3,2,1,0:T(8,128)(2,1)S(1)}, bf16[8,1,8,128]{3,2,1,0:T(8,128)(2,1)S(1)}, u32[]{:S(2)}, u32[]{:S(2)}) %collective-permute-start.27) | collective-permute-done | bytes 16416 | tf_op jit(solution)/shard_map/ppermute | solution.py:11
  490.7 11.6 %all_gather.18 = bf16[16,8,8,128]{3,2,1,0:T(8,128)(2,1)S(1)} all-gather(bf16[16,1,8,128]{3,2,1,0:T(8,128)(2,1)S(1)} %bitcast.198), channel_id=1, replica_groups=mesh['row'=64,'col'=8] {'col'}, dimensions={1}, use_global_device_ids=true | all-gather | bytes 294912 | tf_op jit(solution)/shard_map/all_gather | solution.py:47
  511.0 4.9 collective-permute-done.29
  517.2 11.6 %all_gather.19 = bf16[16,8,8,128]{3,2,1,0:T(8,128)(2,1)S(1)} all-gather(bf16[16,1,8,128]{3,2,1,0:T(8,128)(2,1)S(1)} %subtract_convert_fusion), channel_id=1, replica_groups=mesh['row'=64,'col'=8] {'col'}, dimensions={1}, use_global_device_ids=true | all-gather | bytes 294912 | tf_op jit(solution)/shard_map/all_gather | solution.py:47
  537.5 4.9 collective-permute-done.31
  (158 shorter events, 178.5 us)
Async XLA Ops:
  7.2 132.9 %all-reduce.11.cloned.1.call-start = ((), (), s32[]{:S(2)}) async-start(), calls=%async_computation | async-start | bytes 1048576
  13.4 8.3 %collective-permute-start.1 = (bf16[16,2,8,128]{3,2,1,0:T(8,128)(2,1)S(1)}, bf16[16,2,8,128]{3,2,1,0:T(8,128)(2,1)S(1)}, u32[]{:S(2)}, u32[]{:S(2)}) collective-permute-start(bf16[16,2,8,128]{3,2,1,0:T(8,128)(2,1)S(1)} %maximum_select_fusion.5), channel_id=1, source_target_pairs={{0,16},{8,24},{16,0},{24,8},{32,48},{40,56},{48,32},{56,40},{64,80... | collective-permute-start | bytes 196616 | tf_op jit(solution)/shard_map/ppermute | solution.py:11
  52.2 6.3 %collective-permute-start.2 = (bf16[16,1,8,128]{3,2,1,0:T(8,128)(2,1)S(1)}, bf16[16,1,8,128]{3,2,1,0:T(8,128)(2,1)S(1)}, u32[]{:S(2)}, u32[]{:S(2)}) collective-permute-start(bf16[16,1,8,128]{3,2,1,0:T(8,128)(2,1)S(1)} %dynamic-slice_convert_fusion.5), channel_id=1, source_target_pairs={{0,8},{8,0},{16,24},{24,16},{32,40},{40,32},{48,56},{56,48},{64,72... | collective-permute-start | bytes 98312 | tf_op jit(solution)/shard_map/ppermute | solution.py:11
  58.5 7.1 %collective-permute-start.3 = (bf16[16,2,8,128]{3,2,1,0:T(8,128)(2,1)S(1)}, bf16[16,2,8,128]{3,2,1,0:T(8,128)(2,1)S(1)}, u32[]{:S(2)}, u32[]{:S(2)}) collective-permute-start(bf16[16,2,8,128]{3,2,1,0:T(8,128)(2,1)S(1)} %maximum_select_fusion.6), channel_id=1, source_target_pairs={{0,16},{8,24},{16,0},{24,8},{32,48},{40,56},{48,32},{56,40},{64,80... | collective-permute-start | bytes 196616 | tf_op jit(solution)/shard_map/ppermute | solution.py:11
  66.9 230.8 %all-reduce.13.cloned.1.call-start = ((), (), s32[]{:S(2)}) async-start(), calls=%async_computation.1 | async-start | bytes 524288
  141.6 9.5 %collective-permute-start.4 = (bf16[8,1,8,128]{3,2,1,0:T(8,128)(2,1)S(1)}, bf16[8,1,8,128]{3,2,1,0:T(8,128)(2,1)S(1)}, u32[]{:S(2)}, u32[]{:S(2)}) collective-permute-start(bf16[8,1,8,128]{3,2,1,0:T(8,128)(2,1)S(1)} %dynamic-slice_convert_fusion.13), channel_id=1, source_target_pairs={{0,32},{8,40},{16,48},{24,56},{32,0},{40,8},{48,16},{56,24},{64,96... | collective-permute-start | bytes 49160 | tf_op jit(solution)/shard_map/ppermute | solution.py:11
  156.8 6.7 %collective-permute-start.6 = (bf16[8,2,8,128]{3,2,1,0:T(8,128)(2,1)S(1)}, bf16[8,2,8,128]{3,2,1,0:T(8,128)(2,1)S(1)}, u32[]{:S(2)}, u32[]{:S(2)}) collective-permute-start(bf16[8,2,8,128]{3,2,1,0:T(8,128)(2,1)S(1)} %maximum_select_fusion.10), channel_id=1, source_target_pairs={{0,16},{8,24},{16,0},{24,8},{32,48},{40,56},{48,32},{56,40},{64,80... | collective-permute-start | bytes 98312 | tf_op jit(solution)/shard_map/ppermute | solution.py:11
  163.5 10.1 %collective-permute-start.7 = (bf16[8,4,8,128]{3,2,1,0:T(8,128)(2,1)S(1)}, bf16[8,4,8,128]{3,2,1,0:T(8,128)(2,1)S(1)}, u32[]{:S(2)}, u32[]{:S(2)}) collective-permute-start(bf16[8,4,8,128]{3,2,1,0:T(8,128)(2,1)S(1)} %maximum_select_fusion.7), channel_id=1, source_target_pairs={{0,32},{8,40},{16,48},{24,56},{32,0},{40,8},{48,16},{56,24},{64,96... | collective-permute-start | bytes 196616 | tf_op jit(solution)/shard_map/ppermute | solution.py:11
  206.6 6.7 %collective-permute-start.9 = (bf16[8,2,8,128]{3,2,1,0:T(8,128)(2,1)S(1)}, bf16[8,2,8,128]{3,2,1,0:T(8,128)(2,1)S(1)}, u32[]{:S(2)}, u32[]{:S(2)}) collective-permute-start(bf16[8,2,8,128]{3,2,1,0:T(8,128)(2,1)S(1)} %maximum_select_fusion.11), channel_id=1, source_target_pairs={{0,16},{8,24},{16,0},{24,8},{32,48},{40,56},{48,32},{56,40},{64,80... | collective-permute-start | bytes 98312 | tf_op jit(solution)/shard_map/ppermute | solution.py:11
  213.3 10.1 %collective-permute-start.10 = (bf16[8,4,8,128]{3,2,1,0:T(8,128)(2,1)S(1)}, bf16[8,4,8,128]{3,2,1,0:T(8,128)(2,1)S(1)}, u32[]{:S(2)}, u32[]{:S(2)}) collective-permute-start(bf16[8,4,8,128]{3,2,1,0:T(8,128)(2,1)S(1)} %maximum_select_fusion.8), channel_id=1, source_target_pairs={{0,32},{8,40},{16,48},{24,56},{32,0},{40,8},{48,16},{56,24},{64,96... | collective-permute-start | bytes 196616 | tf_op jit(solution)/shard_map/ppermute | solution.py:11
  310.4 6.7 %collective-permute-start.13 = (bf16[4,2,8,128]{3,2,1,0:T(8,128)(2,1)S(1)}, bf16[4,2,8,128]{3,2,1,0:T(8,128)(2,1)S(1)}, u32[]{:S(2)}, u32[]{:S(2)}) collective-permute-start(bf16[4,2,8,128]{3,2,1,0:T(8,128)(2,1)S(1)} %maximum_select_fusion.14), channel_id=1, source_target_pairs={{0,16},{8,24},{16,0},{24,8},{32,48},{40,56},{48,32},{56,40},{64,80... | collective-permute-start | bytes 49160 | tf_op jit(solution)/shard_map/ppermute | solution.py:11
  317.1 9.7 %collective-permute-start.14 = (bf16[4,4,8,128]{3,2,1,0:T(8,128)(2,1)S(1)}, bf16[4,4,8,128]{3,2,1,0:T(8,128)(2,1)S(1)}, u32[]{:S(2)}, u32[]{:S(2)}) collective-permute-start(bf16[4,4,8,128]{3,2,1,0:T(8,128)(2,1)S(1)} %maximum_select_fusion.12), channel_id=1, source_target_pairs={{0,32},{8,40},{16,48},{24,56},{32,0},{40,8},{48,16},{56,24},{64,96... | collective-permute-start | bytes 98312 | tf_op jit(solution)/shard_map/ppermute | solution.py:11
  374.7 6.3 %collective-permute-start.16 = (bf16[4,8,8,128]{3,2,1,0:T(8,128)(2,1)S(1)}, bf16[4,8,8,128]{3,2,1,0:T(8,128)(2,1)}, u32[]{:S(2)}, u32[]{:S(2)}) collective-permute-start(bf16[4,8,8,128]{3,2,1,0:T(8,128)(2,1)S(1)} %fusion), channel_id=1, source_target_pairs={{0,8},{8,0},{16,24},{24,16},{32,40},{40,32},{48,56},{56,48},{64,72... | collective-permute-start | bytes 196616 | tf_op jit(solution)/shard_map/ppermute | solution.py:11
  381.9 7.1 %collective-permute-start.17 = (bf16[4,4,8,128]{3,2,1,0:T(8,128)(2,1)S(1)}, bf16[4,4,8,128]{3,2,1,0:T(8,128)(2,1)S(1)}, u32[]{:S(2)}, u32[]{:S(2)}) collective-permute-start(bf16[4,4,8,128]{3,2,1,0:T(8,128)(2,1)S(1)} %fusion.6), channel_id=1, source_target_pairs={{0,16},{8,24},{16,0},{24,8},{32,48},{40,56},{48,32},{56,40},{64,80... | collective-permute-start | bytes 98312 | tf_op jit(solution)/shard_map/ppermute | solution.py:11
  389.0 9.5 %collective-permute-start.18 = (bf16[4,2,8,128]{3,2,1,0:T(8,128)(2,1)S(1)}, bf16[4,2,8,128]{3,2,1,0:T(8,128)(2,1)S(1)}, u32[]{:S(2)}, u32[]{:S(2)}) collective-permute-start(bf16[4,2,8,128]{3,2,1,0:T(8,128)(2,1)S(1)} %fusion.11), channel_id=1, source_target_pairs={{0,32},{8,40},{16,48},{24,56},{32,0},{40,8},{48,16},{56,24},{64,96... | collective-permute-start | bytes 49160 | tf_op jit(solution)/shard_map/ppermute | solution.py:11
  421.9 6.2 %collective-permute-start.21 = (bf16[8,4,8,128]{3,2,1,0:T(8,128)(2,1)S(1)}, bf16[8,4,8,128]{3,2,1,0:T(8,128)(2,1)S(1)}, u32[]{:S(2)}, u32[]{:S(2)}) collective-permute-start(bf16[8,4,8,128]{3,2,1,0:T(8,128)(2,1)S(1)} %fusion.1), channel_id=1, source_target_pairs={{0,8},{8,0},{16,24},{24,16},{32,40},{40,32},{48,56},{56,48},{64,72... | collective-permute-start | bytes 196616 | tf_op jit(solution)/shard_map/ppermute | solution.py:11
  428.2 7.0 %collective-permute-start.22 = (bf16[8,2,8,128]{3,2,1,0:T(8,128)(2,1)S(1)}, bf16[8,2,8,128]{3,2,1,0:T(8,128)(2,1)S(1)}, u32[]{:S(2)}, u32[]{:S(2)}) collective-permute-start(bf16[8,2,8,128]{3,2,1,0:T(8,128)(2,1)S(1)} %fusion.7), channel_id=1, source_target_pairs={{0,16},{8,24},{16,0},{24,8},{32,48},{40,56},{48,32},{56,40},{64,80... | collective-permute-start | bytes 98312 | tf_op jit(solution)/shard_map/ppermute | solution.py:11
  435.3 9.5 %collective-permute-start.23 = (bf16[8,1,8,128]{3,2,1,0:T(8,128)(2,1)S(1)}, bf16[8,1,8,128]{3,2,1,0:T(8,128)(2,1)S(1)}, u32[]{:S(2)}, u32[]{:S(2)}) collective-permute-start(bf16[8,1,8,128]{3,2,1,0:T(8,128)(2,1)S(1)} %dynamic-slice_convert_fusion.11), channel_id=1, source_target_pairs={{0,32},{8,40},{16,48},{24,56},{32,0},{40,8},{48,16},{56,24},{64,96... | collective-permute-start | bytes 49160 | tf_op jit(solution)/shard_map/ppermute | solution.py:11
  457.9 6.2 %collective-permute-start.24 = (bf16[8,4,8,128]{3,2,1,0:T(8,128)(2,1)S(1)}, bf16[8,4,8,128]{3,2,1,0:T(8,128)(2,1)S(1)}, u32[]{:S(2)}, u32[]{:S(2)}) collective-permute-start(bf16[8,4,8,128]{3,2,1,0:T(8,128)(2,1)S(1)} %fusion.2), channel_id=1, source_target_pairs={{0,8},{8,0},{16,24},{24,16},{32,40},{40,32},{48,56},{56,48},{64,72... | collective-permute-start | bytes 196616 | tf_op jit(solution)/shard_map/ppermute | solution.py:11
  464.2 6.8 %collective-permute-start.25 = (bf16[8,2,8,128]{3,2,1,0:T(8,128)(2,1)S(1)}, bf16[8,2,8,128]{3,2,1,0:T(8,128)(2,1)S(1)}, u32[]{:S(2)}, u32[]{:S(2)}) collective-permute-start(bf16[8,2,8,128]{3,2,1,0:T(8,128)(2,1)S(1)} %fusion.5), channel_id=1, source_target_pairs={{0,16},{8,24},{16,0},{24,8},{32,48},{40,56},{48,32},{56,40},{64,80... | collective-permute-start | bytes 98312 | tf_op jit(solution)/shard_map/ppermute | solution.py:11
  471.0 9.5 %collective-permute-start.26 = (bf16[8,1,8,128]{3,2,1,0:T(8,128)(2,1)S(1)}, bf16[8,1,8,128]{3,2,1,0:T(8,128)(2,1)S(1)}, u32[]{:S(2)}, u32[]{:S(2)}) collective-permute-start(bf16[8,1,8,128]{3,2,1,0:T(8,128)(2,1)S(1)} %dynamic-slice_convert_fusion.10), channel_id=1, source_target_pairs={{0,32},{8,40},{16,48},{24,56},{32,0},{40,8},{48,16},{56,24},{64,96... | collective-permute-start | bytes 49160 | tf_op jit(solution)/shard_map/ppermute | solution.py:11
  481.1 9.5 %collective-permute-start.27 = (bf16[8,1,8,128]{3,2,1,0:T(8,128)(2,1)S(1)}, bf16[8,1,8,128]{3,2,1,0:T(8,128)(2,1)S(1)}, u32[]{:S(2)}, u32[]{:S(2)}) collective-permute-start(bf16[8,1,8,128]{3,2,1,0:T(8,128)(2,1)S(1)} %get-tuple-element.4), channel_id=1, source_target_pairs={{0,32},{8,40},{16,48},{24,56},{32,0},{40,8},{48,16},{56,24},{64,96... | collective-permute-start | bytes 49160 | tf_op jit(solution)/shard_map/ppermute | solution.py:11
  509.0 6.8 %collective-permute-start.29 = (bf16[16,1,8,128]{3,2,1,0:T(8,128)(2,1)S(1)}, bf16[16,1,8,128]{3,2,1,0:T(8,128)(2,1)S(1)}, u32[]{:S(2)}, u32[]{:S(2)}) collective-permute-start(bf16[16,1,8,128]{3,2,1,0:T(8,128)(2,1)S(1)} %dynamic-slice_convert_fusion.7), channel_id=1, source_target_pairs={{0,16},{8,24},{16,0},{24,8},{32,48},{40,56},{48,32},{56,40},{64,80... | collective-permute-start | bytes 98312 | tf_op jit(solution)/shard_map/ppermute | solution.py:11
  535.6 6.8 %collective-permute-start.31 = (bf16[16,1,8,128]{3,2,1,0:T(8,128)(2,1)S(1)}, bf16[16,1,8,128]{3,2,1,0:T(8,128)(2,1)S(1)}, u32[]{:S(2)}, u32[]{:S(2)}) collective-permute-start(bf16[16,1,8,128]{3,2,1,0:T(8,128)(2,1)S(1)} %dynamic-slice_convert_fusion.6), channel_id=1, source_target_pairs={{0,16},{8,24},{16,0},{24,8},{32,48},{40,56},{48,32},{56,40},{64,80... | collective-permute-start | bytes 98312 | tf_op jit(solution)/shard_map/ppermute | solution.py:11
  (18 other events, 240.7 us)
Sparse Core Ops, SparseCore 0:
  67.0 73.0 all-reduce.10
  225.6 71.9 all-reduce.12
where the time goes:
time: 552 us; the launch traced here: 550 us
  waiting for transfers between devices  261 us (47%)
  blocking collectives  138 us (25%)
  starting transfers between devices  104 us (19%)
  local copies, waits for them, and re-layouts  17.1 us (3%)
  between operations  14.9 us (3%)
  other arithmetic  7.5 us (1%)
  matrix products  7.2 us (1%)
    unnamed x4, waiting for transfers between devices  145 us
    ppermute x32, waiting for transfers between devices, partner(): lax.ppermute(value, axis, [(i, i ^ 1 << stride) for i in range(lax.axis_s...  116 us
    ppermute x32, starting transfers between devices, partner(): lax.ppermute(value, axis, [(i, i ^ 1 << stride) for i in range(lax.axis_s...  104 us
    unnamed x3, blocking collectives  80.7 us
    all_gather x5, blocking collectives, column_join(): gathered = lax.all_gather(pieces, 'col', axis=1, tiled=True)  57 us
  transfers between devices with their start and end apart: 34, of which 33 were waited for; matrix products, arithmetic and copies ran while one was open for 2% of the time, Pallas kernels for 0%

commit v1 on v0

v1 whole, which is shorter than its diff:
```python
import jax
import jax.numpy as jnp
from jax import lax
from jax.sharding import PartitionSpec as P

MB = 64
GR = 4


def row_groups(row_devs, group):
    return [[first + r for r in range(group)] for first in range(0, row_devs, group)]


def family_groups(row_devs, col_devs, group):
    return [
        [(first + s * group + r) * col_devs + c for s in range(2) for c in range(col_devs)]
        for first in range(0, row_devs, 2 * group)
        for r in range(group)
    ]


def exchange(slots, axis, groups=None):
    return lax.all_to_all(slots, axis, 0, 0, axis_index_groups=groups, tiled=True)


def share(piece, count, axis, groups=None):
    slots = lax.optimization_barrier(jnp.broadcast_to(piece[None], (count,) + piece.shape))
    return exchange(slots, axis, groups)


def coupling(values, listings, group):
    row_blocks = values.shape[0] // MB
    position = lax.axis_index("row")
    owned = jnp.arange(row_blocks, dtype=jnp.int32) * group + position % group
    listing = lax.dynamic_index_in_dim(listings, position // group, 0, keepdims=False)
    listed = jnp.any(listing[None, :, :] == owned[:, None, None], axis=-1)
    unit_width = values.shape[1] // listed.shape[1]
    keeping = jnp.repeat(jnp.repeat(listed, MB, axis=0), unit_width, axis=1)
    return jnp.where(keeping, values, jnp.zeros_like(values))


def per_device(dinv0, dinv1, dinv2, offdiag0, offdiag1, rhs0, rhs1, rhs2, block_rows0, block_rows1):
    row_devs = lax.axis_size("row")
    col_devs = lax.axis_size("col")
    unit = MB // col_devs
    width = rhs0.shape[1]
    groups = (GR, 2 * GR, 4 * GR)
    inverses = (dinv0, dinv1, dinv2)
    couplings = (coupling(offdiag0, block_rows0, groups[0]), coupling(offdiag1, block_rows1, groups[1]))
    sides = (rhs0, rhs1, rhs2)
    own = [row_groups(row_devs, group) for group in groups]
    family = [family_groups(row_devs, col_devs, group) for group in groups[:2]]

    def column_form(piece, level):
        gathered = share(piece, groups[level], "row", own[level])
        return gathered.transpose(1, 0, 2, 3).reshape(-1, width)

    def apply_plain(matrix, vector):
        return jnp.dot(matrix, vector, preferred_element_type=jnp.float32)

    def apply_transposed(matrix, vector):
        return jnp.einsum("ij,in->jn", matrix, vector, preferred_element_type=jnp.float32)

    def total(slots):
        return jnp.sum(slots.astype(jnp.float32), axis=0)

    solved = []
    residual = rhs0.reshape(-1, unit, width)
    for level in range(3):
        product = apply_plain(inverses[level], column_form(residual, level)).astype(jnp.bfloat16)
        if level == 2:
            shared = share(product, col_devs, "col")
            break
        slots = product.reshape(-1, col_devs, unit, width).transpose(1, 0, 2, 3)
        piece = total(exchange(slots, "col")).astype(jnp.bfloat16)
        solved.append(piece)
        partial_value = apply_plain(couplings[level], column_form(piece, level)).astype(jnp.bfloat16)
        slots = partial_value.reshape(-1, 2, col_devs, unit, width).transpose(1, 2, 0, 3, 4)
        slots = slots.reshape(2 * col_devs, -1, unit, width)
        update = total(exchange(slots, ("row", "col"), family[level]))
        side = sides[level + 1].reshape(-1, unit, width).astype(jnp.float32)
        residual = (side - update).astype(jnp.bfloat16)

    def row_sum(product, level):
        slots = product.astype(jnp.bfloat16).reshape(-1, groups[level], unit, width)
        return total(exchange(slots.transpose(1, 0, 2, 3), "row", own[level]))

    outputs = [None, None, None]
    row_form = total(shared).astype(jnp.bfloat16)
    for level in (2, 1, 0):
        answer = row_sum(apply_transposed(inverses[level], row_form), level)
        outputs[level] = answer.reshape(-1, width)
        if level > 0:
            child = level - 1
            gathered = share(answer.astype(jnp.bfloat16), 2 * col_devs, ("row", "col"), family[child])
            gathered = gathered.reshape(2, col_devs, -1, unit, width).transpose(2, 0, 1, 3, 4)
            carried = row_sum(apply_transposed(couplings[child], gathered.reshape(-1, width)), child)
            weighted = (solved[child].astype(jnp.float32) - carried).astype(jnp.bfloat16)
            gathered = share(weighted, col_devs, "col")
            row_form = gathered.transpose(1, 0, 2, 3).reshape(-1, width)
    return (outputs[0], outputs[1], outputs[2])


def solution(mesh):
    placed = (
        P("row", "col"),
        P("row", "col"),
        P("row", "col"),
        P("row", "col"),
        P("row", "col"),
        P(("row", "col"), None),
        P(("row", "col"), None),
        P(("row", "col"), None),
        P(),
        P(),
    )
    return jax.shard_map(
        per_device,
        mesh=mesh,
        in_specs=placed,
        out_specs=(P(("row", "col"), None), P(("row", "col"), None), P(("row", "col"), None)),
        check_vma=False,
    )
```

time: 552 us -> 234 us (0.42)
  the two profiles are of different devices: /device:TPU:24 before, /device:TPU:128 now
where the time goes in v1:
time: 234 us; the launch traced here: 233 us
  blocking collectives  175 us (75%)
  waiting for transfers between devices  24.5 us (10%)
  starting transfers between devices  14.5 us (6%)
  local copies, waits for them, and re-layouts  11.3 us (5%)
  matrix products  4.58 us (2%)
    all_to_all x15, blocking collectives, exchange(): lax.all_to_all(slots, axis, 0, 0, axis_index_groups=groups, tiled=True)  175 us
    all_to_all x4, waiting for transfers between devices, exchange(): lax.all_to_all(slots, axis, 0, 0, axis_index_groups=groups, tiled=True)  24.5 us
    all_to_all x4, starting transfers between devices, exchange(): lax.all_to_all(slots, axis, 0, 0, axis_index_groups=groups, tiled=True)  14.5 us
  transfers between devices with their start and end apart: 4, of which 4 were waited for; matrix products, arithmetic and copies ran while one was open for 2% of the time, Pallas kernels for 0%

profile of v1, /device:TPU:128, one launch (start us, length us, event | category | flops | bytes accessed | tf_op | source)
XLA Modules:
  0.0 232.7 jit_solution(15843046413998394245)
XLA Ops:
  1.5 10.7 %all_to_all.95 = bf16[4,16,8,128]{3,2,1,0:T(8,128)(2,1)S(1)} all-to-all(bf16[4,16,8,128]{3,2,1,0:T(8,128)(2,1)S(1)} %broadcast_in_dim.35), channel_id=1, replica_groups={{0,8,16,24},{32,40,48,56},{64,72,80,88},{96,104,112,120},{128,136,144,1..., dimensions={0} | all-to-all | bytes 262144 | tf_op jit(solution)/shard_map/all_to_all | solution.py:23
  13.5 4.3 %all-to-all-start.1 = ((bf16[8,16,8,128]{3,2,1,0:T(8,128)(2,1)}), bf16[8,16,8,128]{3,2,1,0:T(8,128)(2,1)S(1)}, u32[]{:S(2)}, u32[]{:S(2)}) async-start(bf16[8,16,8,128]{3,2,1,0:T(8,128)(2,1)} %bitcast.112), calls=%async_computation.1 | async-start | bytes 524288 | tf_op jit(solution)/shard_map/all_to_all | solution.py:23
  18.5 6.8 %all-to-all-done.1 = bf16[8,16,8,128]{3,2,1,0:T(8,128)(2,1)S(1)} async-done(((bf16[8,16,8,128]{3,2,1,0:T(8,128)(2,1)}), bf16[8,16,8,128]{3,2,1,0:T(8,128)(2,1)S(1)}, u32[]{:S(2)}, u32[]{:S(2)}) %all-to-all-start.1) | async-done | bytes 262176 | tf_op jit(solution)/shard_map/all_to_all | solution.py:23
  26.0 3.3 %all-to-all-start.2 = ((bf16[4,16,8,128]{3,2,1,0:T(8,128)(2,1)}), bf16[4,16,8,128]{3,2,1,0:T(8,128)(2,1)S(1)}, u32[]{:S(2)}, u32[]{:S(2)}) async-start(bf16[4,16,8,128]{3,2,1,0:T(8,128)(2,1)} %broadcast_in_dim.39), calls=%async_computation.2 | async-start | bytes 262144 | tf_op jit(solution)/shard_map/all_to_all | solution.py:23
  30.5 4.8 %all-to-all-done.2 = bf16[4,16,8,128]{3,2,1,0:T(8,128)(2,1)S(1)} async-done(((bf16[4,16,8,128]{3,2,1,0:T(8,128)(2,1)}), bf16[4,16,8,128]{3,2,1,0:T(8,128)(2,1)S(1)}, u32[]{:S(2)}, u32[]{:S(2)}) %all-to-all-start.2) | async-done | bytes 131104 | tf_op jit(solution)/shard_map/all_to_all | solution.py:23
  36.1 17.5 %all_to_all.96 = bf16[16,8,8,128]{3,2,1,0:T(8,128)(2,1)S(1)} all-to-all(bf16[16,8,8,128]{3,2,1,0:T(8,128)(2,1)S(1)} %bitcast.115), channel_id=1, replica_groups={{0,1,2,3,4,5,6,7,32,33,34,35,36,37,38,39},{8,9,10,11,12,13,14,15,40,41,..., dimensions={0} | all-to-all | bytes 524288 | tf_op jit(solution)/shard_map/all_to_all | solution.py:23
  53.6 14.1 %all_to_all.97 = bf16[8,8,8,128]{3,2,1,0:T(8,128)(2,1)S(1)} all-to-all(bf16[8,8,8,128]{3,2,1,0:T(8,128)(2,1)S(1)} %broadcast_in_dim.40), channel_id=1, replica_groups={{0,8,16,24,32,40,48,56},{64,72,80,88,96,104,112,120},{128,136,144,152,1..., dimensions={0} | all-to-all | bytes 262144 | tf_op jit(solution)/shard_map/all_to_all | solution.py:23
  68.9 3.5 %all-to-all-start.5 = ((bf16[8,8,8,128]{3,2,1,0:T(8,128)(2,1)}), bf16[8,8,8,128]{3,2,1,0:T(8,128)(2,1)S(1)}, u32[]{:S(2)}, u32[]{:S(2)}) async-start(bf16[8,8,8,128]{3,2,1,0:T(8,128)(2,1)} %copy.58), calls=%async_computation.5 | async-start | bytes 262144 | tf_op jit(solution)/shard_map/all_to_all | solution.py:23
  72.4 6.0 %all-to-all-done.5 = bf16[8,8,8,128]{3,2,1,0:T(8,128)(2,1)S(1)} async-done(((bf16[8,8,8,128]{3,2,1,0:T(8,128)(2,1)}), bf16[8,8,8,128]{3,2,1,0:T(8,128)(2,1)S(1)}, u32[]{:S(2)}, u32[]{:S(2)}) %all-to-all-start.5) | async-done | bytes 131104 | tf_op jit(solution)/shard_map/all_to_all | solution.py:23
  79.1 3.4 %all-to-all-start.6 = ((bf16[8,8,8,128]{3,2,1,0:T(8,128)(2,1)}), bf16[8,8,8,128]{3,2,1,0:T(8,128)(2,1)S(1)}, u32[]{:S(2)}, u32[]{:S(2)}) async-start(bf16[8,8,8,128]{3,2,1,0:T(8,128)(2,1)} %broadcast_in_dim.44), calls=%async_computation.6 | async-start | bytes 262144 | tf_op jit(solution)/shard_map/all_to_all | solution.py:23
  84.7 6.8 %all-to-all-done.6 = bf16[8,8,8,128]{3,2,1,0:T(8,128)(2,1)S(1)} async-done(((bf16[8,8,8,128]{3,2,1,0:T(8,128)(2,1)}), bf16[8,8,8,128]{3,2,1,0:T(8,128)(2,1)S(1)}, u32[]{:S(2)}, u32[]{:S(2)}) %all-to-all-start.6) | async-done | bytes 131104 | tf_op jit(solution)/shard_map/all_to_all | solution.py:23
  91.6 1.4 convolution_convert_fusion.4
  93.1 10.8 %all_to_all.98 = bf16[16,4,8,128]{3,2,1,0:T(8,128)(2,1)S(1)} all-to-all(bf16[16,4,8,128]{3,2,1,0:T(8,128)(2,1)S(1)} %bitcast.120), channel_id=1, replica_groups={{0,1,2,3,4,5,6,7,64,65,66,67,68,69,70,71},{8,9,10,11,12,13,14,15,72,73,..., dimensions={0} | all-to-all | bytes 262144 | tf_op jit(solution)/shard_map/all_to_all | solution.py:23
  104.6 11.6 %all_to_all.99 = bf16[16,4,8,128]{3,2,1,0:T(8,128)(2,1)S(1)} all-to-all(bf16[16,4,8,128]{3,2,1,0:T(8,128)(2,1)S(1)} %broadcast_in_dim.45), channel_id=1, replica_groups={{0,8,16,24,32,40,48,56,64,72,80,88,96,104,112,120},{128,136,144,152,160..., dimensions={0} | all-to-all | bytes 262144 | tf_op jit(solution)/shard_map/all_to_all | solution.py:23
  116.7 12.8 %all_to_all.100 = bf16[8,256,128]{2,1,0:T(8,128)(2,1)S(1)} all-to-all(bf16[8,256,128]{2,1,0:T(8,128)(2,1)S(1)} %broadcast_in_dim.46), channel_id=1, replica_groups=mesh['row'=64,'col'=8] {'col'}, dimensions={0} | all-to-all | bytes 1048576 | tf_op jit(solution)/shard_map/all_to_all | solution.py:23
  129.9 11.8 %all_to_all.101 = bf16[16,4,8,128]{3,2,1,0:T(8,128)(2,1)S(1)} all-to-all(bf16[16,4,8,128]{3,2,1,0:T(8,128)(2,1)S(1)} %copy.66), channel_id=1, replica_groups={{0,8,16,24,32,40,48,56,64,72,80,88,96,104,112,120},{128,136,144,152,160..., dimensions={0} | all-to-all | bytes 262144 | tf_op jit(solution)/shard_map/all_to_all | solution.py:23
  142.3 9.3 %all_to_all.102 = bf16[16,4,8,128]{3,2,1,0:T(8,128)(2,1)S(1)} all-to-all(bf16[16,4,8,128]{3,2,1,0:T(8,128)(2,1)S(1)} %broadcast_in_dim.47), channel_id=1, replica_groups={{0,1,2,3,4,5,6,7,64,65,66,67,68,69,70,71},{8,9,10,11,12,13,14,15,72,73,..., dimensions={0} | all-to-all | bytes 262144 | tf_op jit(solution)/shard_map/all_to_all | solution.py:23
  152.1 11.9 %all_to_all.103 = bf16[8,8,8,128]{3,2,1,0:T(8,128)(2,1)S(1)} all-to-all(bf16[8,8,8,128]{3,2,1,0:T(8,128)(2,1)S(1)} %bitcast.122), channel_id=1, replica_groups={{0,8,16,24,32,40,48,56},{64,72,80,88,96,104,112,120},{128,136,144,152,1..., dimensions={0} | all-to-all | bytes 262144 | tf_op jit(solution)/shard_map/all_to_all | solution.py:23
  164.0 8.5 %all_to_all.104 = bf16[8,8,8,128]{3,2,1,0:T(8,128)(2,1)S(1)} all-to-all(bf16[8,8,8,128]{3,2,1,0:T(8,128)(2,1)S(1)} %broadcast_in_dim.48), channel_id=1, replica_groups=mesh['row'=64,'col'=8] {'col'}, dimensions={0} | all-to-all | bytes 262144 | tf_op jit(solution)/shard_map/all_to_all | solution.py:23
  173.0 11.5 %all_to_all.105 = bf16[8,8,8,128]{3,2,1,0:T(8,128)(2,1)S(1)} all-to-all(bf16[8,8,8,128]{3,2,1,0:T(8,128)(2,1)S(1)} %copy.71), channel_id=1, replica_groups={{0,8,16,24,32,40,48,56},{64,72,80,88,96,104,112,120},{128,136,144,152,1..., dimensions={0} | all-to-all | bytes 262144 | tf_op jit(solution)/shard_map/all_to_all | solution.py:23
  185.2 14.7 %all_to_all.106 = bf16[16,8,8,128]{3,2,1,0:T(8,128)(2,1)S(1)} all-to-all(bf16[16,8,8,128]{3,2,1,0:T(8,128)(2,1)S(1)} %broadcast_in_dim.98), channel_id=1, replica_groups={{0,1,2,3,4,5,6,7,32,33,34,35,36,37,38,39},{8,9,10,11,12,13,14,15,40,41,..., dimensions={0} | all-to-all | bytes 524288 | tf_op jit(solution)/shard_map/all_to_all | solution.py:23
  201.2 11.7 %all_to_all.107 = bf16[4,16,8,128]{3,2,1,0:T(8,128)(2,1)S(1)} all-to-all(bf16[4,16,8,128]{3,2,1,0:T(8,128)(2,1)S(1)} %bitcast.124), channel_id=1, replica_groups={{0,8,16,24},{32,40,48,56},{64,72,80,88},{96,104,112,120},{128,136,144,1..., dimensions={0} | all-to-all | bytes 262144 | tf_op jit(solution)/shard_map/all_to_all | solution.py:23
  212.9 9.9 %all_to_all.108 = bf16[8,16,8,128]{3,2,1,0:T(8,128)(2,1)S(1)} all-to-all(bf16[8,16,8,128]{3,2,1,0:T(8,128)(2,1)S(1)} %broadcast_in_dim.99), channel_id=1, replica_groups=mesh['row'=64,'col'=8] {'col'}, dimensions={0} | all-to-all | bytes 524288 | tf_op jit(solution)/shard_map/all_to_all | solution.py:23
  223.4 8.6 %all_to_all.109 = bf16[4,16,8,128]{3,2,1,0:T(8,128)(2,1)S(1)} all-to-all(bf16[4,16,8,128]{3,2,1,0:T(8,128)(2,1)S(1)} %copy.76), channel_id=1, replica_groups={{0,8,16,24},{32,40,48,56},{64,72,80,88},{96,104,112,120},{128,136,144,1..., dimensions={0} | all-to-all | bytes 262144 | tf_op jit(solution)/shard_map/all_to_all | solution.py:23
  (96 shorter events, 15.7 us)
Async XLA Ops:
  0.6 11.7 %copy-start = (bf16[1024,512]{1,0:T(8,128)(2,1)S(1)}, bf16[1024,512]{1,0:T(8,128)(2,1)}, u32[]{:S(2)}) copy-start(bf16[1024,512]{1,0:T(8,128)(2,1)} %param.10) | copy-start | bytes 3145732
  12.7 17.2 %copy-start.3 = (bf16[1024,512]{1,0:T(8,128)(2,1)S(1)}, bf16[1024,512]{1,0:T(8,128)(2,1)}, u32[]{:S(2)}) copy-start(bf16[1024,512]{1,0:T(8,128)(2,1)} %param.13) | copy-start | bytes 3145732
  13.5 11.8 %all-to-all-start.1 = ((bf16[8,16,8,128]{3,2,1,0:T(8,128)(2,1)}), bf16[8,16,8,128]{3,2,1,0:T(8,128)(2,1)S(1)}, u32[]{:S(2)}, u32[]{:S(2)}) async-start(bf16[8,16,8,128]{3,2,1,0:T(8,128)(2,1)} %bitcast.112), calls=%async_computation.1 | async-start | bytes 524288 | tf_op jit(solution)/shard_map/all_to_all | solution.py:23
  26.0 9.4 %all-to-all-start.2 = ((bf16[4,16,8,128]{3,2,1,0:T(8,128)(2,1)}), bf16[4,16,8,128]{3,2,1,0:T(8,128)(2,1)S(1)}, u32[]{:S(2)}, u32[]{:S(2)}) async-start(bf16[4,16,8,128]{3,2,1,0:T(8,128)(2,1)} %broadcast_in_dim.39), calls=%async_computation.2 | async-start | bytes 262144 | tf_op jit(solution)/shard_map/all_to_all | solution.py:23
  30.0 5.4 %copy-start.7 = (pred[1024,64]{0,1:T(8,128)(4,1)}, pred[1024,64]{0,1:T(8,128)(4,1)S(1)}, u32[]{:S(2)}) copy-start(pred[1024,64]{0,1:T(8,128)(4,1)S(1)} %reshape.153) | copy-start | bytes 196612
  36.1 17.5 %copy-start.10 = (bf16[64,128]{1,0:T(8,128)(2,1)S(1)}, bf16[64,128]{1,0:T(8,128)(2,1)}, u32[]{:S(2)}) copy-start(bf16[64,128]{1,0:T(8,128)(2,1)} %param.16) | copy-start | bytes 49156
  53.5 14.2 %copy-start.1 = (bf16[512,512]{1,0:T(8,128)(2,1)S(1)}, bf16[512,512]{1,0:T(8,128)(2,1)}, u32[]{:S(2)}) copy-start(bf16[512,512]{1,0:T(8,128)(2,1)} %param.11) | copy-start | bytes 1572868
  68.9 14.8 %copy-start.4 = (bf16[512,512]{1,0:T(8,128)(2,1)S(1)}, bf16[512,512]{1,0:T(8,128)(2,1)}, u32[]{:S(2)}) copy-start(bf16[512,512]{1,0:T(8,128)(2,1)} %param.14) | copy-start | bytes 1572868
  68.9 9.5 %all-to-all-start.5 = ((bf16[8,8,8,128]{3,2,1,0:T(8,128)(2,1)}), bf16[8,8,8,128]{3,2,1,0:T(8,128)(2,1)S(1)}, u32[]{:S(2)}, u32[]{:S(2)}) async-start(bf16[8,8,8,128]{3,2,1,0:T(8,128)(2,1)} %copy.58), calls=%async_computation.5 | async-start | bytes 262144 | tf_op jit(solution)/shard_map/all_to_all | solution.py:23
  79.1 12.5 %all-to-all-start.6 = ((bf16[8,8,8,128]{3,2,1,0:T(8,128)(2,1)}), bf16[8,8,8,128]{3,2,1,0:T(8,128)(2,1)S(1)}, u32[]{:S(2)}, u32[]{:S(2)}) async-start(bf16[8,8,8,128]{3,2,1,0:T(8,128)(2,1)} %broadcast_in_dim.44), calls=%async_computation.6 | async-start | bytes 262144 | tf_op jit(solution)/shard_map/all_to_all | solution.py:23
  103.9 0.7 copy-start.11
  104.6 11.6 %copy-start.2 = (bf16[256,512]{1,0:T(8,128)(2,1)S(1)}, bf16[256,512]{1,0:T(8,128)(2,1)}, u32[]{:S(2)}) copy-start(bf16[256,512]{1,0:T(8,128)(2,1)} %param.12) | copy-start | bytes 786436
  129.9 21.8 %copy-start.5 = (bf16[512,512]{0,1:T(8,128)(2,1)S(1)}, bf16[512,512]{0,1:T(8,128)(2,1)}, u32[]{:S(2)}) copy-start(bf16[512,512]{0,1:T(8,128)(2,1)} %copy.60) | copy-start | bytes 1572868
  141.7 0.6 copy-start.9
  184.5 0.6 copy-start.6
  199.8 0.8 copy-start.8

commit v2 on v1

v2 whole, which is shorter than its diff:
```python
import jax
import jax.numpy as jnp
from jax import lax
from jax.sharding import PartitionSpec as P

MB = 64
GR = 4


def row_groups(row_devs, group):
    return [[first + r for r in range(group)] for first in range(0, row_devs, group)]


def family_groups(row_devs, col_devs, group):
    return [
        [(first + s * group + r) * col_devs + c for s in range(2) for c in range(col_devs)]
        for first in range(0, row_devs, 2 * group)
        for r in range(group)
    ]


def exchange(slots, axis, groups=None):
    return lax.all_to_all(slots, axis, 0, 0, axis_index_groups=groups, tiled=True)


def share(piece, count, axis, groups=None):
    slots = lax.optimization_barrier(jnp.broadcast_to(piece[None], (count,) + piece.shape))
    return exchange(slots, axis, groups)


def coupling(values, listings, group):
    row_blocks = values.shape[0] // MB
    position = lax.axis_index("row")
    owned = jnp.arange(row_blocks, dtype=jnp.int32) * group + position % group
    listing = lax.dynamic_index_in_dim(listings, position // group, 0, keepdims=False)
    listed = jnp.any(listing[None, :, :] == owned[:, None, None], axis=-1)
    blocks = listed.shape[1]
    columns = lax.broadcasted_iota(jnp.int32, (blocks, values.shape[1]), 1) // (values.shape[1] // blocks)
    spread = (columns == lax.broadcasted_iota(jnp.int32, columns.shape, 0)).astype(jnp.bfloat16)
    keeping = jnp.dot(listed.astype(jnp.bfloat16), spread, preferred_element_type=jnp.float32) > 0.5
    shaped = values.reshape(row_blocks, MB, -1)
    return jnp.where(keeping[:, None, :], shaped, jnp.zeros_like(shaped)).reshape(values.shape)


def per_device(dinv0, dinv1, dinv2, offdiag0, offdiag1, rhs0, rhs1, rhs2, block_rows0, block_rows1):
    row_devs = lax.axis_size("row")
    col_devs = lax.axis_size("col")
    unit = MB // col_devs
    width = rhs0.shape[1]
    groups = (GR, 2 * GR, 4 * GR)
    inverses = (dinv0, dinv1, dinv2)
    own = [row_groups(row_devs, group) for group in groups]
    family = family_groups(row_devs, col_devs, groups[1])
    half = lax.axis_index("row") // groups[0] % 2

    def apply_plain(matrix, vector):
        return jnp.dot(matrix, vector, preferred_element_type=jnp.float32).astype(jnp.bfloat16)

    def apply_transposed(matrix, vector):
        product = jnp.einsum("ij,in->jn", matrix, vector, preferred_element_type=jnp.float32)
        return product.astype(jnp.bfloat16)

    def total(slots):
        return jnp.sum(slots.astype(jnp.float32), axis=0)

    def row_gather(piece, level):
        return share(piece, groups[level], "row", own[level])

    def flat(gathered):
        return gathered.transpose(1, 0, 2, 3).reshape(-1, width)

    def column_sum(product):
        slots = product.reshape(-1, col_devs, unit, width).transpose(1, 0, 2, 3)
        return total(exchange(slots, "col"))

    def row_sum(product, level):
        slots = product.reshape(-1, groups[level], unit, width).transpose(1, 0, 2, 3)
        return total(exchange(slots, "row", own[level]))

    mine = lax.broadcasted_iota(jnp.int32, (1, 2, 1, 1), 1) == half
    gathered, coupled0, coupled1, side1, side2 = lax.optimization_barrier(
        (
            row_gather(rhs0.reshape(-1, unit, width), 0),
            coupling(offdiag0, block_rows0, groups[0]),
            coupling(offdiag1, block_rows1, groups[1]),
            jnp.where(mine, rhs1.reshape(-1, 1, unit, width).astype(jnp.float32), 0.0),
            rhs2.reshape(-1, unit, width).astype(jnp.float32),
        )
    )
    solved0 = column_sum(apply_plain(dinv0, flat(gathered))).astype(jnp.bfloat16)
    update = column_sum(apply_plain(coupled0, flat(row_gather(solved0, 0))))
    update = update.reshape(-1, 2, unit, width)
    gathered = row_gather((side1 - update).astype(jnp.bfloat16), 1)
    gathered = gathered.reshape(2, groups[0], -1, unit, width)
    residual = total(gathered).astype(jnp.bfloat16)

    solved1 = column_sum(apply_plain(dinv1, flat(residual))).astype(jnp.bfloat16)
    partial_value = apply_plain(coupled1, flat(row_gather(solved1, 1)))
    slots = partial_value.reshape(-1, 2, col_devs, unit, width).transpose(1, 2, 0, 3, 4)
    slots = slots.reshape(2 * col_devs, -1, unit, width)
    update = total(exchange(slots, ("row", "col"), family))
    residual = (side2 - update).astype(jnp.bfloat16)

    shared = share(apply_plain(dinv2, flat(row_gather(residual, 2))), col_devs, "col")
    row_form = total(shared).astype(jnp.bfloat16)
    answer2 = row_sum(apply_transposed(dinv2, row_form), 2)

    gathered = share(answer2.astype(jnp.bfloat16), 2 * col_devs, ("row", "col"), family)
    gathered = gathered.reshape(2, col_devs, -1, unit, width).transpose(2, 0, 1, 3, 4)
    carried = row_sum(apply_transposed(coupled1, gathered.reshape(-1, width)), 1)
    weighted = (solved1.astype(jnp.float32) - carried).astype(jnp.bfloat16)
    product = apply_transposed(dinv1, flat(share(weighted, col_devs, "col")))
    slots = product.reshape(-1, 2, groups[0], unit, width).transpose(2, 0, 1, 3, 4)
    slots = jnp.broadcast_to(slots[None], (2,) + slots.shape).reshape(groups[1], -1, unit, width)
    both = total(exchange(slots, "row", own[1]))
    pairs = both.reshape(-1, 2, unit, width)
    answer1 = jnp.where(half == 0, pairs[:, 0], pairs[:, 1])
    both, answer1 = lax.optimization_barrier((both, answer1))

    child_form = flat(share(both.astype(jnp.bfloat16), col_devs, "col"))
    carried = row_sum(apply_transposed(coupled0, child_form), 0)
    weighted = (solved0.astype(jnp.float32) - carried).astype(jnp.bfloat16)
    answer0 = row_sum(apply_transposed(dinv0, flat(share(weighted, col_devs, "col"))), 0)
    return tuple(answer.reshape(-1, width) for answer in (answer0, answer1, answer2))


def solution(mesh):
    placed = (
        P("row", "col"),
        P("row", "col"),
        P("row", "col"),
        P("row", "col"),
        P("row", "col"),
        P(("row", "col"), None),
        P(("row", "col"), None),
        P(("row", "col"), None),
        P(),
        P(),
    )
    return jax.shard_map(
        per_device,
        mesh=mesh,
        in_specs=placed,
        out_specs=(P(("row", "col"), None), P(("row", "col"), None), P(("row", "col"), None)),
        check_vma=False,
    )
```

time: 234 us -> 224 us (0.957)
  waiting for transfers between devices: 24.5 us -> 14.4 us
  starting transfers between devices: 14.5 us -> 8.28 us
  blocking collectives: 175 us -> 181 us
  other arithmetic: 1.2 us -> 4.4 us
  local copies, waits for them, and re-layouts: 11.3 us -> 8.52 us
    all_to_all x4 -> x2, waiting for transfers between devices: 24.5 us -> 14.4 us  [exchange(): lax.all_to_all(slots, axis, 0, 0, axis_index_groups=groups, tiled=True)]
    all_to_all x4 -> x2, starting transfers between devices: 14.5 us -> 8.28 us  [exchange(): lax.all_to_all(slots, axis, 0, 0, axis_index_groups=groups, tiled=True)]
    all_to_all x15 -> x17, blocking collectives: 175 us -> 181 us  [exchange(): lax.all_to_all(slots, axis, 0, 0, axis_index_groups=groups, tiled=True)]
  transfers between devices with their start and end apart: 4 -> 2, of which waited for: 4 -> 2; matrix products, arithmetic and copies ran while one was open for 2% -> 1% of each run, Pallas kernels for 0% -> 0%
where the time goes in v2:
time: 224 us; the launch traced here: 222 us
  blocking collectives  181 us (81%)
  waiting for transfers between devices  14.4 us (6%)
  local copies, waits for them, and re-layouts  8.52 us (4%)
  starting transfers between devices  8.28 us (4%)
  matrix products  4.52 us (2%)
  other arithmetic  4.4 us (2%)
    all_to_all x17, blocking collectives, exchange(): lax.all_to_all(slots, axis, 0, 0, axis_index_groups=groups, tiled=True)  181 us
    all_to_all x2, waiting for transfers between devices, exchange(): lax.all_to_all(slots, axis, 0, 0, axis_index_groups=groups, tiled=True)  14.4 us
    all_to_all x2, starting transfers between devices, exchange(): lax.all_to_all(slots, axis, 0, 0, axis_index_groups=groups, tiled=True)  8.28 us
  transfers between devices with their start and end apart: 2, of which 2 were waited for; matrix products, arithmetic and copies ran while one was open for 1% of the time, Pallas kernels for 0%

profile of v2, /device:TPU:128, one launch (start us, length us, event | category | flops | bytes accessed | tf_op | source)
XLA Modules:
  0.0 222.5 jit_solution(13256347392537473592)
XLA Ops:
  0.7 1.5 broadcast_in_dim.69
  2.2 4.9 %all-to-all-start = ((bf16[4,16,8,128]{3,2,1,0:T(8,128)(2,1)}), bf16[4,16,8,128]{3,2,1,0:T(8,128)(2,1)S(1)}, u32[]{:S(2)}, u32[]{:S(2)}) async-start(bf16[4,16,8,128]{3,2,1,0:T(8,128)(2,1)} %broadcast_in_dim.69), calls=%async_computation | async-start | bytes 262144 | tf_op jit(solution)/shard_map/all_to_all | solution.py:23
  10.6 2.5 %all-to-all-done = bf16[4,16,8,128]{3,2,1,0:T(8,128)(2,1)S(1)} async-done(((bf16[4,16,8,128]{3,2,1,0:T(8,128)(2,1)}), bf16[4,16,8,128]{3,2,1,0:T(8,128)(2,1)S(1)}, u32[]{:S(2)}, u32[]{:S(2)}) %all-to-all-start) | async-done | bytes 131104 | tf_op jit(solution)/shard_map/all_to_all | solution.py:23
  13.9 11.6 %all_to_all.95 = bf16[8,16,8,128]{3,2,1,0:T(8,128)(2,1)S(1)} all-to-all(bf16[8,16,8,128]{3,2,1,0:T(8,128)(2,1)S(1)} %copy.51), channel_id=1, replica_groups=mesh['row'=64,'col'=8] {'col'}, dimensions={0} | all-to-all | bytes 524288 | tf_op jit(solution)/shard_map/all_to_all | solution.py:23
  26.1 8.5 %all_to_all.96 = bf16[4,16,8,128]{3,2,1,0:T(8,128)(2,1)S(1)} all-to-all(bf16[4,16,8,128]{3,2,1,0:T(8,128)(2,1)S(1)} %broadcast_in_dim.130), channel_id=1, replica_groups={{0,8,16,24},{32,40,48,56},{64,72,80,88},{96,104,112,120},{128,136,144,1..., dimensions={0} | all-to-all | bytes 262144 | tf_op jit(solution)/shard_map/all_to_all | solution.py:23
  35.2 9.9 %all_to_all.97 = bf16[8,16,8,128]{3,2,1,0:T(8,128)(2,1)S(1)} all-to-all(bf16[8,16,8,128]{3,2,1,0:T(8,128)(2,1)S(1)} %bitcast.118), channel_id=1, replica_groups=mesh['row'=64,'col'=8] {'col'}, dimensions={0} | all-to-all | bytes 524288 | tf_op jit(solution)/shard_map/all_to_all | solution.py:23
  45.2 17.1 %all_to_all.98 = bf16[8,8,2,8,128]{4,3,2,1,0:T(8,128)(2,1)S(1)} all-to-all(bf16[8,8,2,8,128]{4,3,2,1,0:T(8,128)(2,1)S(1)} %broadcast_in_dim.131), channel_id=1, replica_groups={{0,8,16,24,32,40,48,56},{64,72,80,88,96,104,112,120},{128,136,144,152,1..., dimensions={0} | all-to-all | bytes 524288 | tf_op jit(solution)/shard_map/all_to_all | solution.py:23
  62.9 8.5 %all_to_all.99 = bf16[8,8,8,128]{3,2,1,0:T(8,128)(2,1)S(1)} all-to-all(bf16[8,8,8,128]{3,2,1,0:T(8,128)(2,1)S(1)} %copy.56), channel_id=1, replica_groups=mesh['row'=64,'col'=8] {'col'}, dimensions={0} | all-to-all | bytes 262144 | tf_op jit(solution)/shard_map/all_to_all | solution.py:23
  71.5 11.5 %all_to_all.100 = bf16[8,8,8,128]{3,2,1,0:T(8,128)(2,1)S(1)} all-to-all(bf16[8,8,8,128]{3,2,1,0:T(8,128)(2,1)S(1)} %broadcast_in_dim.132), channel_id=1, replica_groups={{0,8,16,24,32,40,48,56},{64,72,80,88,96,104,112,120},{128,136,144,152,1..., dimensions={0} | all-to-all | bytes 262144 | tf_op jit(solution)/shard_map/all_to_all | solution.py:23
  83.4 10.8 %all_to_all.101 = bf16[16,4,8,128]{3,2,1,0:T(8,128)(2,1)S(1)} all-to-all(bf16[16,4,8,128]{3,2,1,0:T(8,128)(2,1)S(1)} %bitcast.127), channel_id=1, replica_groups={{0,1,2,3,4,5,6,7,64,65,66,67,68,69,70,71},{8,9,10,11,12,13,14,15,72,73,..., dimensions={0} | all-to-all | bytes 262144 | tf_op jit(solution)/shard_map/all_to_all | solution.py:23
  94.9 11.6 %all_to_all.102 = bf16[16,4,8,128]{3,2,1,0:T(8,128)(2,1)S(1)} all-to-all(bf16[16,4,8,128]{3,2,1,0:T(8,128)(2,1)S(1)} %broadcast_in_dim.133), channel_id=1, replica_groups={{0,8,16,24,32,40,48,56,64,72,80,88,96,104,112,120},{128,136,144,152,160..., dimensions={0} | all-to-all | bytes 262144 | tf_op jit(solution)/shard_map/all_to_all | solution.py:23
  107.0 13.4 %all_to_all.103 = bf16[8,256,128]{2,1,0:T(8,128)(2,1)} all-to-all(bf16[8,256,128]{2,1,0:T(8,128)(2,1)S(1)} %broadcast_in_dim.134), channel_id=1, replica_groups=mesh['row'=64,'col'=8] {'col'}, dimensions={0} | all-to-all | bytes 1048576 | tf_op jit(solution)/shard_map/all_to_all | solution.py:23
  120.5 1.8 reduce_sum.116
  122.2 1.0 fusion.3
  123.4 11.6 %all_to_all.104 = bf16[16,4,8,128]{3,2,1,0:T(8,128)(2,1)S(1)} all-to-all(bf16[16,4,8,128]{3,2,1,0:T(8,128)(2,1)S(1)} %copy.62), channel_id=1, replica_groups={{0,8,16,24,32,40,48,56,64,72,80,88,96,104,112,120},{128,136,144,152,160..., dimensions={0} | all-to-all | bytes 262144 | tf_op jit(solution)/shard_map/all_to_all | solution.py:23
  135.7 9.3 %all_to_all.105 = bf16[16,4,8,128]{3,2,1,0:T(8,128)(2,1)S(1)} all-to-all(bf16[16,4,8,128]{3,2,1,0:T(8,128)(2,1)S(1)} %broadcast_in_dim.135), channel_id=1, replica_groups={{0,1,2,3,4,5,6,7,64,65,66,67,68,69,70,71},{8,9,10,11,12,13,14,15,72,73,..., dimensions={0} | all-to-all | bytes 262144 | tf_op jit(solution)/shard_map/all_to_all | solution.py:23
  145.4 11.9 %all_to_all.106 = bf16[8,8,8,128]{3,2,1,0:T(8,128)(2,1)S(1)} all-to-all(bf16[8,8,8,128]{3,2,1,0:T(8,128)(2,1)S(1)} %bitcast.129), channel_id=1, replica_groups={{0,8,16,24,32,40,48,56},{64,72,80,88,96,104,112,120},{128,136,144,152,1..., dimensions={0} | all-to-all | bytes 262144 | tf_op jit(solution)/shard_map/all_to_all | solution.py:23
  157.4 8.5 %all_to_all.107 = bf16[8,8,8,128]{3,2,1,0:T(8,128)(2,1)S(1)} all-to-all(bf16[8,8,8,128]{3,2,1,0:T(8,128)(2,1)S(1)} %broadcast_in_dim.136), channel_id=1, replica_groups=mesh['row'=64,'col'=8] {'col'}, dimensions={0} | all-to-all | bytes 262144 | tf_op jit(solution)/shard_map/all_to_all | solution.py:23
  167.0 3.4 %all-to-all-start.14 = ((bf16[8,16,8,128]{3,2,1,0:T(8,128)(2,1)}), bf16[8,16,8,128]{3,2,1,0:T(8,128)(2,1)S(1)}, u32[]{:S(2)}, u32[]{:S(2)}) async-start(bf16[8,16,8,128]{3,2,1,0:T(8,128)(2,1)} %bitcast.44), calls=%async_computation.14 | async-start | bytes 524288 | tf_op jit(solution)/shard_map/all_to_all | solution.py:23
  170.4 11.9 %all-to-all-done.14 = bf16[8,16,8,128]{3,2,1,0:T(8,128)(2,1)S(1)} async-done(((bf16[8,16,8,128]{3,2,1,0:T(8,128)(2,1)}), bf16[8,16,8,128]{3,2,1,0:T(8,128)(2,1)S(1)}, u32[]{:S(2)}, u32[]{:S(2)}) %all-to-all-start.14) | async-done | bytes 262176 | tf_op jit(solution)/shard_map/all_to_all | solution.py:23
  183.0 9.9 %all_to_all.108 = bf16[8,16,8,128]{3,2,1,0:T(8,128)(2,1)S(1)} all-to-all(bf16[8,16,8,128]{3,2,1,0:T(8,128)(2,1)S(1)} %broadcast_in_dim.138), channel_id=1, replica_groups=mesh['row'=64,'col'=8] {'col'}, dimensions={0} | all-to-all | bytes 524288 | tf_op jit(solution)/shard_map/all_to_all | solution.py:23
  193.5 8.5 %all_to_all.109 = bf16[4,16,8,128]{3,2,1,0:T(8,128)(2,1)S(1)} all-to-all(bf16[4,16,8,128]{3,2,1,0:T(8,128)(2,1)S(1)} %bitcast.131), channel_id=1, replica_groups={{0,8,16,24},{32,40,48,56},{64,72,80,88},{96,104,112,120},{128,136,144,1..., dimensions={0} | all-to-all | bytes 262144 | tf_op jit(solution)/shard_map/all_to_all | solution.py:23
  202.8 9.9 %all_to_all.110 = bf16[8,16,8,128]{3,2,1,0:T(8,128)(2,1)S(1)} all-to-all(bf16[8,16,8,128]{3,2,1,0:T(8,128)(2,1)S(1)} %broadcast_in_dim.139), channel_id=1, replica_groups=mesh['row'=64,'col'=8] {'col'}, dimensions={0} | all-to-all | bytes 524288 | tf_op jit(solution)/shard_map/all_to_all | solution.py:23
  213.3 8.5 %all_to_all.111 = bf16[4,16,8,128]{3,2,1,0:T(8,128)(2,1)S(1)} all-to-all(bf16[4,16,8,128]{3,2,1,0:T(8,128)(2,1)S(1)} %copy.72), channel_id=1, replica_groups={{0,8,16,24},{32,40,48,56},{64,72,80,88},{96,104,112,120},{128,136,144,1..., dimensions={0} | all-to-all | bytes 262144 | tf_op jit(solution)/shard_map/all_to_all | solution.py:23
  (98 shorter events, 13.1 us)
Async XLA Ops:
  0.6 12.5 %copy-start = (bf16[1024,512]{1,0:T(8,128)(2,1)S(1)}, bf16[1024,512]{1,0:T(8,128)(2,1)}, u32[]{:S(2)}) copy-start(bf16[1024,512]{1,0:T(8,128)(2,1)} %param.10) | copy-start | bytes 3145732
  0.6 8.6 %copy-start.4 = (bf16[512,512]{1,0:T(8,128)(2,1)S(1)}, bf16[512,512]{1,0:T(8,128)(2,1)}, u32[]{:S(2)}) copy-start(bf16[512,512]{1,0:T(8,128)(2,1)} %param.14) | copy-start | bytes 1572868
  2.2 10.9 %all-to-all-start = ((bf16[4,16,8,128]{3,2,1,0:T(8,128)(2,1)}), bf16[4,16,8,128]{3,2,1,0:T(8,128)(2,1)S(1)}, u32[]{:S(2)}, u32[]{:S(2)}) async-start(bf16[4,16,8,128]{3,2,1,0:T(8,128)(2,1)} %broadcast_in_dim.69), calls=%async_computation | async-start | bytes 262144 | tf_op jit(solution)/shard_map/all_to_all | solution.py:23
  7.1 2.1 copy-start.9
  7.2 2.2 copy-start.3
  9.3 0.7 copy-start.10
  25.5 0.6 copy-start.5
  45.2 17.2 %copy-start.1 = (bf16[512,512]{1,0:T(8,128)(2,1)S(1)}, bf16[512,512]{1,0:T(8,128)(2,1)}, u32[]{:S(2)}) copy-start(bf16[512,512]{1,0:T(8,128)(2,1)} %param.11) | copy-start | bytes 1572868
  94.2 0.7 copy-start.8
  94.9 11.6 %copy-start.2 = (bf16[256,512]{1,0:T(8,128)(2,1)S(1)}, bf16[256,512]{1,0:T(8,128)(2,1)}, u32[]{:S(2)}) copy-start(bf16[256,512]{1,0:T(8,128)(2,1)} %param.12) | copy-start | bytes 786436
  135.0 0.6 copy-start.7
  167.0 15.3 %all-to-all-start.14 = ((bf16[8,16,8,128]{3,2,1,0:T(8,128)(2,1)}), bf16[8,16,8,128]{3,2,1,0:T(8,128)(2,1)S(1)}, u32[]{:S(2)}, u32[]{:S(2)}) async-start(bf16[8,16,8,128]{3,2,1,0:T(8,128)(2,1)} %bitcast.44), calls=%async_computation.14 | async-start | bytes 524288 | tf_op jit(solution)/shard_map/all_to_all | solution.py:23
  202.0 0.8 copy-start.6

commit v3 on v2

--- a/solution.py
+++ b/solution.py
@@ -1,6 +1,8 @@
 import jax
 import jax.numpy as jnp
 from jax import lax
+from jax.experimental import pallas as pl
+from jax.experimental.pallas import tpu as pltpu
 from jax.sharding import PartitionSpec as P
 
 MB = 64
@@ -28,7 +30,7 @@
     return exchange(slots, axis, groups)
 
 
-def coupling(values, listings, group):
+def kept(values, listings, group):
     row_blocks = values.shape[0] // MB
     position = lax.axis_index("row")
     owned = jnp.arange(row_blocks, dtype=jnp.int32) * group + position % group
@@ -37,9 +39,51 @@
     blocks = listed.shape[1]
     columns = lax.broadcasted_iota(jnp.int32, (blocks, values.shape[1]), 1) // (values.shape[1] // blocks)
     spread = (columns == lax.broadcasted_iota(jnp.int32, columns.shape, 0)).astype(jnp.bfloat16)
-    keeping = jnp.dot(listed.astype(jnp.bfloat16), spread, preferred_element_type=jnp.float32) > 0.5
-    shaped = values.reshape(row_blocks, MB, -1)
+    return jnp.dot(listed.astype(jnp.bfloat16), spread, preferred_element_type=jnp.float32) > 0.5
+
+
+def coupling(values, keeping):
+    shaped = values.reshape(keeping.shape[0], MB, -1)
     return jnp.where(keeping[:, None, :], shaped, jnp.zeros_like(shaped)).reshape(values.shape)
+
+
+def coupled_transposed(values_ref, kept_ref, vector_ref, slots_ref, sums_ref):
+    step = pl.program_id(0)
+    shaped = values_ref[...].reshape(kept_ref.shape[0], MB, -1) * kept_ref[...]
+    product = lax.dot_general(
+        shaped.reshape(values_ref.shape),
+        vector_ref[...],
+        (((0,), (0,)), ((), ())),
+        preferred_element_type=jnp.float32,
+    )
+    sums_ref[...] = jnp.where(step == 0, product, sums_ref[...] + product)
+
+    @pl.when(step == pl.num_programs(0) - 1)
+    def _():
+        blocks, group, unit, width = slots_ref.shape[1], slots_ref.shape[0], slots_ref.shape[2], slots_ref.shape[3]
+        sums = sums_ref[...].reshape(blocks, group, unit, width)
+        for r in range(group):
+            slots_ref[r] = sums[:, r].astype(slots_ref.dtype)
+
+
+def coupled_slots(values, keeping, vector, group, unit, steps=4):
+    rows, columns = values.shape
+    width = vector.shape[1]
+    blocks = columns // (group * unit)
+    held = rows // MB // steps
+    return pl.pallas_call(
+        coupled_transposed,
+        grid=(steps,),
+        in_specs=[
+            pl.BlockSpec((rows // steps, columns), lambda i: (i, 0)),
+            pl.BlockSpec((held, 1, columns), lambda i: (i, 0, 0)),
+            pl.BlockSpec((rows // steps, width), lambda i: (i, 0)),
+        ],
+        out_specs=pl.BlockSpec((group, blocks, unit, width), lambda i: (0, 0, 0, 0)),
+        out_shape=jax.ShapeDtypeStruct((group, blocks, unit, width), jnp.bfloat16),
+        scratch_shapes=[pltpu.VMEM((columns, width), jnp.float32)],
+        name="coupled_transposed",
+    )(values, keeping[:, None, :].astype(jnp.bfloat16), vector)
 
 
 def per_device(dinv0, dinv1, dinv2, offdiag0, offdiag1, rhs0, rhs1, rhs2, block_rows0, block_rows1):
@@ -78,24 +122,27 @@
         return total(exchange(slots, "row", own[level]))
 
     mine = lax.broadcasted_iota(jnp.int32, (1, 2, 1, 1), 1) == half
-    gathered, coupled0, coupled1, side1, side2 = lax.optimization_barrier(
+    gathered, kept0, kept1, side1, side2, first = lax.optimization_barrier(
         (
             row_gather(rhs0.reshape(-1, unit, width), 0),
-            coupling(offdiag0, block_rows0, groups[0]),
-            coupling(offdiag1, block_rows1, groups[1]),
+            kept(offdiag0, block_rows0, groups[0]),
+            kept(offdiag1, block_rows1, groups[1]),
             jnp.where(mine, rhs1.reshape(-1, 1, unit, width).astype(jnp.float32), 0.0),
             rhs2.reshape(-1, unit, width).astype(jnp.float32),
+            half == 0,
         )
     )
     solved0 = column_sum(apply_plain(dinv0, flat(gathered))).astype(jnp.bfloat16)
-    update = column_sum(apply_plain(coupled0, flat(row_gather(solved0, 0))))
+    gathered, kept0 = lax.optimization_barrier((row_gather(solved0, 0), kept0))
+    update = column_sum(apply_plain(coupling(offdiag0, kept0), flat(gathered)))
     update = update.reshape(-1, 2, unit, width)
     gathered = row_gather((side1 - update).astype(jnp.bfloat16), 1)
     gathered = gathered.reshape(2, groups[0], -1, unit, width)
     residual = total(gathered).astype(jnp.bfloat16)
 
     solved1 = column_sum(apply_plain(dinv1, flat(residual))).astype(jnp.bfloat16)
-    partial_value = apply_plain(coupled1, flat(row_gather(solved1, 1)))
+    gathered, kept1 = lax.optimization_barrier((row_gather(solved1, 1), kept1))
+    partial_value = apply_plain(coupling(offdiag1, kept1), flat(gathered))
     slots = partial_value.reshape(-1, 2, col_devs, unit, width).transpose(1, 2, 0, 3, 4)
     slots = slots.reshape(2 * col_devs, -1, unit, width)
     update = total(exchange(slots, ("row", "col"), family))
@@ -106,19 +153,21 @@
     answer2 = row_sum(apply_transposed(dinv2, row_form), 2)
 
     gathered = share(answer2.astype(jnp.bfloat16), 2 * col_devs, ("row", "col"), family)
+    gathered, kept1 = lax.optimization_barrier((gathered, kept1))
     gathered = gathered.reshape(2, col_devs, -1, unit, width).transpose(2, 0, 1, 3, 4)
-    carried = row_sum(apply_transposed(coupled1, gathered.reshape(-1, width)), 1)
+    carried = row_sum(apply_transposed(coupling(offdiag1, kept1), gathered.reshape(-1, width)), 1)
     weighted = (solved1.astype(jnp.float32) - carried).astype(jnp.bfloat16)
     product = apply_transposed(dinv1, flat(share(weighted, col_devs, "col")))
     slots = product.reshape(-1, 2, groups[0], unit, width).transpose(2, 0, 1, 3, 4)
     slots = jnp.broadcast_to(slots[None], (2,) + slots.shape).reshape(groups[1], -1, unit, width)
     both = total(exchange(slots, "row", own[1]))
     pairs = both.reshape(-1, 2, unit, width)
-    answer1 = jnp.where(half == 0, pairs[:, 0], pairs[:, 1])
+    answer1 = jnp.where(first, pairs[:, 0], pairs[:, 1])
     both, answer1 = lax.optimization_barrier((both, answer1))
 
-    child_form = flat(share(both.astype(jnp.bfloat16), col_devs, "col"))
-    carried = row_sum(apply_transposed(coupled0, child_form), 0)
+    gathered, kept0 = lax.optimization_barrier((share(both.astype(jnp.bfloat16), col_devs, "col"), kept0))
+    slots = coupled_slots(offdiag0, kept0, flat(gathered), groups[0], unit)
+    carried = total(exchange(slots, "row", own[0]))
     weighted = (solved0.astype(jnp.float32) - carried).astype(jnp.bfloat16)
     answer0 = row_sum(apply_transposed(dinv0, flat(share(weighted, col_devs, "col"))), 0)
     return tuple(answer.reshape(-1, width) for answer in (answer0, answer1, answer2))

time: 224 us -> 223 us (level)
  blocking collectives: 181 us -> 196 us
  waiting for transfers between devices: 14.4 us -> 3.31 us
  Pallas kernels: 0 us -> 3.53 us
  starting transfers between devices: 8.28 us -> 4.87 us
    all_to_all x17 -> x18, blocking collectives: 181 us -> 196 us  [exchange(): lax.all_to_all(slots, axis, 0, 0, axis_index_groups=groups, tiled=True)]
    all_to_all x2 -> x1, waiting for transfers between devices: 14.4 us -> 3.31 us  [exchange(): lax.all_to_all(slots, axis, 0, 0, axis_index_groups=groups, tiled=True)]
    pallas_call x0 -> x1, Pallas kernels: none -> 3.53 us  [coupled_slots(): pl.pallas_call(coupled_transposed, grid=(steps,), in_specs=[pl.BlockSpec(...]
    all_to_all x2 -> x1, starting transfers between devices: 8.28 us -> 4.87 us  [exchange(): lax.all_to_all(slots, axis, 0, 0, axis_index_groups=groups, tiled=True)]
  transfers between devices with their start and end apart: 2 -> 1, of which waited for: 2 -> 1; matrix products, arithmetic and copies ran while one was open for 1% -> 1% of each run, Pallas kernels for 0% -> 0%
where the time goes in v3:
time: 223 us; the launch traced here: 221 us
  blocking collectives  196 us (88%)
  local copies, waits for them, and re-layouts  7.11 us (3%)
  starting transfers between devices  4.87 us (2%)
  Pallas kernels  3.53 us (2%)
  waiting for transfers between devices  3.31 us (1%)
  matrix products  3.19 us (1%)
    all_to_all x18, blocking collectives, exchange(): lax.all_to_all(slots, axis, 0, 0, axis_index_groups=groups, tiled=True)  196 us
    all_to_all x1, starting transfers between devices, exchange(): lax.all_to_all(slots, axis, 0, 0, axis_index_groups=groups, tiled=True)  4.87 us
  transfers between devices with their start and end apart: 1, of which 1 were waited for; matrix products, arithmetic and copies ran while one was open for 1% of the time, Pallas kernels for 0%

profile of v3, /device:TPU:128, one launch (start us, length us, event | category | flops | bytes accessed | tf_op | source)
XLA Modules:
  0.0 221.4 jit_solution(14316593432081724255)
XLA Ops:
  0.6 1.5 broadcast_in_dim.74
  2.1 4.9 %all-to-all-start = ((bf16[4,16,8,128]{3,2,1,0:T(8,128)(2,1)}), bf16[4,16,8,128]{3,2,1,0:T(8,128)(2,1)S(1)}, u32[]{:S(2)}, u32[]{:S(2)}) async-start(bf16[4,16,8,128]{3,2,1,0:T(8,128)(2,1)} %broadcast_in_dim.74), calls=%async_computation | async-start | bytes 262144 | tf_op jit(solution)/shard_map/all_to_all | solution.py:25
  8.6 0.7 dynamic-slice_bitcast_fusion
  9.8 3.3 %all-to-all-done = bf16[4,16,8,128]{3,2,1,0:T(8,128)(2,1)S(1)} async-done(((bf16[4,16,8,128]{3,2,1,0:T(8,128)(2,1)}), bf16[4,16,8,128]{3,2,1,0:T(8,128)(2,1)S(1)}, u32[]{:S(2)}, u32[]{:S(2)}) %all-to-all-start) | async-done | bytes 131104 | tf_op jit(solution)/shard_map/all_to_all | solution.py:25
  13.9 11.7 %all_to_all.95 = bf16[8,16,8,128]{3,2,1,0:T(8,128)(2,1)S(1)} all-to-all(bf16[8,16,8,128]{3,2,1,0:T(8,128)(2,1)S(1)} %copy.52), channel_id=1, replica_groups=mesh['row'=64,'col'=8] {'col'}, dimensions={0} | all-to-all | bytes 524288 | tf_op jit(solution)/shard_map/all_to_all | solution.py:25
  25.7 8.6 %all_to_all.96 = bf16[4,16,8,128]{3,2,1,0:T(8,128)(2,1)S(1)} all-to-all(bf16[4,16,8,128]{3,2,1,0:T(8,128)(2,1)S(1)} %broadcast_in_dim.130), channel_id=1, replica_groups={{0,8,16,24},{32,40,48,56},{64,72,80,88},{96,104,112,120},{128,136,144,1..., dimensions={0} | all-to-all | bytes 262144 | tf_op jit(solution)/shard_map/all_to_all | solution.py:25
  34.9 9.9 %all_to_all.97 = bf16[8,16,8,128]{3,2,1,0:T(8,128)(2,1)S(1)} all-to-all(bf16[8,16,8,128]{3,2,1,0:T(8,128)(2,1)S(1)} %bitcast.115), channel_id=1, replica_groups=mesh['row'=64,'col'=8] {'col'}, dimensions={0} | all-to-all | bytes 524288 | tf_op jit(solution)/shard_map/all_to_all | solution.py:25
  44.9 17.1 %all_to_all.98 = bf16[8,8,2,8,128]{4,3,2,1,0:T(8,128)(2,1)S(1)} all-to-all(bf16[8,8,2,8,128]{4,3,2,1,0:T(8,128)(2,1)S(1)} %broadcast_in_dim.134), channel_id=1, replica_groups={{0,8,16,24,32,40,48,56},{64,72,80,88,96,104,112,120},{128,136,144,152,1..., dimensions={0} | all-to-all | bytes 524288 | tf_op jit(solution)/shard_map/all_to_all | solution.py:25
  62.6 8.6 %all_to_all.99 = bf16[8,8,8,128]{3,2,1,0:T(8,128)(2,1)S(1)} all-to-all(bf16[8,8,8,128]{3,2,1,0:T(8,128)(2,1)S(1)} %copy.57), channel_id=1, replica_groups=mesh['row'=64,'col'=8] {'col'}, dimensions={0} | all-to-all | bytes 262144 | tf_op jit(solution)/shard_map/all_to_all | solution.py:25
  71.2 11.5 %all_to_all.100 = bf16[8,8,8,128]{3,2,1,0:T(8,128)(2,1)S(1)} all-to-all(bf16[8,8,8,128]{3,2,1,0:T(8,128)(2,1)S(1)} %broadcast_in_dim.135), channel_id=1, replica_groups={{0,8,16,24,32,40,48,56},{64,72,80,88,96,104,112,120},{128,136,144,152,1..., dimensions={0} | all-to-all | bytes 262144 | tf_op jit(solution)/shard_map/all_to_all | solution.py:25
  83.2 10.8 %all_to_all.101 = bf16[16,4,8,128]{3,2,1,0:T(8,128)(2,1)S(1)} all-to-all(bf16[16,4,8,128]{3,2,1,0:T(8,128)(2,1)S(1)} %bitcast.126), channel_id=1, replica_groups={{0,1,2,3,4,5,6,7,64,65,66,67,68,69,70,71},{8,9,10,11,12,13,14,15,72,73,..., dimensions={0} | all-to-all | bytes 262144 | tf_op jit(solution)/shard_map/all_to_all | solution.py:25
  94.1 11.6 %all_to_all.102 = bf16[16,4,8,128]{3,2,1,0:T(8,128)(2,1)S(1)} all-to-all(bf16[16,4,8,128]{3,2,1,0:T(8,128)(2,1)S(1)} %broadcast_in_dim.138), channel_id=1, replica_groups={{0,8,16,24,32,40,48,56,64,72,80,88,96,104,112,120},{128,136,144,152,160..., dimensions={0} | all-to-all | bytes 262144 | tf_op jit(solution)/shard_map/all_to_all | solution.py:25
  106.2 12.8 %all_to_all.103 = bf16[8,256,128]{2,1,0:T(8,128)(2,1)S(1)} all-to-all(bf16[8,256,128]{2,1,0:T(8,128)(2,1)S(1)} %broadcast_in_dim.139), channel_id=1, replica_groups=mesh['row'=64,'col'=8] {'col'}, dimensions={0} | all-to-all | bytes 1048576 | tf_op jit(solution)/shard_map/all_to_all | solution.py:25
  119.4 11.6 %all_to_all.104 = bf16[16,4,8,128]{3,2,1,0:T(8,128)(2,1)S(1)} all-to-all(bf16[16,4,8,128]{3,2,1,0:T(8,128)(2,1)S(1)} %copy.63), channel_id=1, replica_groups={{0,8,16,24,32,40,48,56,64,72,80,88,96,104,112,120},{128,136,144,152,160..., dimensions={0} | all-to-all | bytes 262144 | tf_op jit(solution)/shard_map/all_to_all | solution.py:25
  131.7 9.3 %all_to_all.105 = bf16[16,4,8,128]{3,2,1,0:T(8,128)(2,1)S(1)} all-to-all(bf16[16,4,8,128]{3,2,1,0:T(8,128)(2,1)S(1)} %broadcast_in_dim.140), channel_id=1, replica_groups={{0,1,2,3,4,5,6,7,64,65,66,67,68,69,70,71},{8,9,10,11,12,13,14,15,72,73,..., dimensions={0} | all-to-all | bytes 262144 | tf_op jit(solution)/shard_map/all_to_all | solution.py:25
  141.5 11.9 %all_to_all.106 = bf16[8,8,8,128]{3,2,1,0:T(8,128)(2,1)S(1)} all-to-all(bf16[8,8,8,128]{3,2,1,0:T(8,128)(2,1)S(1)} %bitcast.128), channel_id=1, replica_groups={{0,8,16,24,32,40,48,56},{64,72,80,88,96,104,112,120},{128,136,144,152,1..., dimensions={0} | all-to-all | bytes 262144 | tf_op jit(solution)/shard_map/all_to_all | solution.py:25
  153.4 8.5 %all_to_all.107 = bf16[8,8,8,128]{3,2,1,0:T(8,128)(2,1)S(1)} all-to-all(bf16[8,8,8,128]{3,2,1,0:T(8,128)(2,1)S(1)} %broadcast_in_dim.143), channel_id=1, replica_groups=mesh['row'=64,'col'=8] {'col'}, dimensions={0} | all-to-all | bytes 262144 | tf_op jit(solution)/shard_map/all_to_all | solution.py:25
  162.4 14.4 %all_to_all.108 = bf16[8,16,8,128]{3,2,1,0:T(8,128)(2,1)S(1)} all-to-all(bf16[8,16,8,128]{3,2,1,0:T(8,128)(2,1)S(1)} %bitcast.117), channel_id=1, replica_groups={{0,8,16,24,32,40,48,56},{64,72,80,88,96,104,112,120},{128,136,144,152,1..., dimensions={0} | all-to-all | bytes 524288 | tf_op jit(solution)/shard_map/all_to_all | solution.py:25
  177.5 9.9 %all_to_all.109 = bf16[8,16,8,128]{3,2,1,0:T(8,128)(2,1)S(1)} all-to-all(bf16[8,16,8,128]{3,2,1,0:T(8,128)(2,1)S(1)} %broadcast_in_dim.145), channel_id=1, replica_groups=mesh['row'=64,'col'=8] {'col'}, dimensions={0} | all-to-all | bytes 524288 | tf_op jit(solution)/shard_map/all_to_all | solution.py:25
  187.4 0.8 copy.69
  188.8 3.5 %coupled_transposed.1 = bf16[4,16,8,128]{3,2,1,0:T(8,128)(2,1)} custom-call(bf16[1024,512]{1,0:T(8,128)(2,1)} %values_ref.1, bf16[16,1,512]{2,1,0:T(2,128)(2,1)} %copy.70.kept_ref, bf16[1024,128]{1,0:T(8,128)(2,1)} %bitcast.119), custom_call_target="tpu_custom_call" | custom-call | tf_op jit(solution)/shard_map/coupled_transposed/pallas_call | solution.py:74
  192.3 9.4 %all_to_all.110 = bf16[4,16,8,128]{3,2,1,0:T(8,128)(2,1)S(1)} all-to-all(bf16[4,16,8,128]{3,2,1,0:T(8,128)(2,1)} %coupled_transposed.1), channel_id=1, replica_groups={{0,8,16,24},{32,40,48,56},{64,72,80,88},{96,104,112,120},{128,136,144,1..., dimensions={0} | all-to-all | bytes 262144 | tf_op jit(solution)/shard_map/all_to_all | solution.py:25
  201.8 9.9 %all_to_all.111 = bf16[8,16,8,128]{3,2,1,0:T(8,128)(2,1)S(1)} all-to-all(bf16[8,16,8,128]{3,2,1,0:T(8,128)(2,1)S(1)} %broadcast_in_dim.146), channel_id=1, replica_groups=mesh['row'=64,'col'=8] {'col'}, dimensions={0} | all-to-all | bytes 524288 | tf_op jit(solution)/shard_map/all_to_all | solution.py:25
  212.3 8.5 %all_to_all.112 = bf16[4,16,8,128]{3,2,1,0:T(8,128)(2,1)S(1)} all-to-all(bf16[4,16,8,128]{3,2,1,0:T(8,128)(2,1)S(1)} %copy.73), channel_id=1, replica_groups={{0,8,16,24},{32,40,48,56},{64,72,80,88},{96,104,112,120},{128,136,144,1..., dimensions={0} | all-to-all | bytes 262144 | tf_op jit(solution)/shard_map/all_to_all | solution.py:25
  (93 shorter events, 9.5 us)
Async XLA Ops:
  0.6 12.5 %copy-start = (bf16[1024,512]{1,0:T(8,128)(2,1)S(1)}, bf16[1024,512]{1,0:T(8,128)(2,1)}, u32[]{:S(2)}) copy-start(bf16[1024,512]{1,0:T(8,128)(2,1)} %param.10) | copy-start | bytes 3145732
  2.1 10.9 %all-to-all-start = ((bf16[4,16,8,128]{3,2,1,0:T(8,128)(2,1)}), bf16[4,16,8,128]{3,2,1,0:T(8,128)(2,1)S(1)}, u32[]{:S(2)}, u32[]{:S(2)}) async-start(bf16[4,16,8,128]{3,2,1,0:T(8,128)(2,1)} %broadcast_in_dim.74), calls=%async_computation | async-start | bytes 262144 | tf_op jit(solution)/shard_map/all_to_all | solution.py:25
  7.0 0.7 copy-start.7
  7.1 0.7 copy-start.6
  13.8 20.5 %copy-start.1 = (bf16[1024,512]{1,0:T(8,128)(2,1)S(1)}, bf16[1024,512]{1,0:T(8,128)(2,1)}, u32[]{:S(2)}) copy-start(bf16[1024,512]{1,0:T(8,128)(2,1)} %values_ref.1) | copy-start | bytes 3145732
  44.9 17.2 %copy-start.2 = (bf16[512,512]{1,0:T(8,128)(2,1)S(1)}, bf16[512,512]{1,0:T(8,128)(2,1)}, u32[]{:S(2)}) copy-start(bf16[512,512]{1,0:T(8,128)(2,1)} %param.11) | copy-start | bytes 1572868
  62.6 20.3 %copy-start.3 = (bf16[512,512]{1,0:T(8,128)(2,1)S(1)}, bf16[512,512]{1,0:T(8,128)(2,1)}, u32[]{:S(2)}) copy-start(bf16[512,512]{1,0:T(8,128)(2,1)} %param.14) | copy-start | bytes 1572868
  94.1 11.6 %copy-start.4 = (bf16[256,512]{1,0:T(8,128)(2,1)S(1)}, bf16[256,512]{1,0:T(8,128)(2,1)}, u32[]{:S(2)}) copy-start(bf16[256,512]{1,0:T(8,128)(2,1)} %param.12) | copy-start | bytes 786436
  131.1 0.6 copy-start.5
